TPU v7x, 128 devices: a whole 4x4x4 slice. The times are simulated.
128 devices in a mesh: sector: 16 (over x, z_lo, core), slab: 8 (over y, z_hi).
Axes of the slice: x: 4, y: 4, z: 4 (z_hi: 2, z_lo: 2; z = z_hi * 2 + z_lo), core: 2. Of those that a mesh axis runs over, the one named last changes fastest.
Arguments:
- right_basis: float32 [64, 128, 96, 256], P(None, 'sector', 'slab')
- left_basis: float32 [64, 128, 96, 256], P(None, 'sector', 'slab')
- speed_squared: float32 [128, 96, 256], P('sector', 'slab'), may hold values from 0.5 to 8
- rayleigh: float32 [64, 64], replicated
- schur_order: int32 [64], replicated, may hold values from 0 to 63, each once
- kept_index: int32 [32], replicated, may hold values from 0 to 63, as said below
- rim_map: int32 [256], replicated, may hold values from 0 to 255, each once
Outputs:
- new_right: float32 [32, 128, 96, 256], P(None, 'sector', 'slab')
- new_left: float32 [32, 128, 96, 256], P(None, 'sector', 'slab')
- right_image: float32 [32, 128, 96, 256], P(None, 'sector', 'slab')
- left_image: float32 [32, 128, 96, 256], P(None, 'sector', 'slab')
- restarted: float32 [32, 32], replicated
Inputs may be any that keep to these rules, and one draw needn't show every extreme that they name: `kept_index`: 32 distinct basis indices, 0 and 63 among them. `schur_order`: each basis index once. `rim_map`: each radial cell once.
All inputs are finite; a program needn't handle non-finite values.
Results may differ from a plain program's by a relative error of at most 0.0003.
Values sent between devices are 32-bit elements; how exact they have to be, the bound alone decides.
A program may use at most 256 MiB of HBM per device.

v0:
```python
import jax
import jax.numpy as jnp
from jax import lax
from jax.sharding import PartitionSpec as P


def padded_2(shard, sides, width, wrap):
    for axis, dim in sides:
        peers, length = (lax.axis_size(axis), shard.shape[dim])
        up = [(i, (i + 1) % peers) for i in range(peers if wrap else peers - 1)]
        down = [(j, i) for i, j in up]
        last = lax.slice_in_dim(shard, length - width, length, axis=dim)
        first = lax.slice_in_dim(shard, 0, width, axis=dim)
        before = lax.ppermute(last, axis, up)
        after = lax.ppermute(first, axis, down)
        shard = jnp.concatenate([before, shard, after], axis=dim)
    return shard


def exact_dot(left_operator, right_operator):
    return jnp.dot(left_operator, right_operator, precision=lax.Precision.HIGHEST)


def lower_inverse(lower_factor):
    identity = jnp.eye(lower_factor.shape[0], dtype=lower_factor.dtype)
    return lax.linalg.triangular_solve(lower_factor, identity, left_side=True, lower=True)


def solve_inverse(cross_matrix):
    normal_matrix = exact_dot(cross_matrix.T, cross_matrix)
    scaling_factor = jnp.linalg.cholesky(normal_matrix)
    middle = lax.linalg.triangular_solve(scaling_factor, cross_matrix.T, left_side=True, lower=True)
    return lax.linalg.triangular_solve(
        scaling_factor, middle, left_side=True, lower=True, transpose_a=True
    )


def orthonormal(matrix):

    def column_step(column_index, partial_basis):
        column_index = jnp.asarray(column_index).astype(jnp.int32)
        column = lax.dynamic_slice_in_dim(matrix, column_index, 1, 1)
        column = column - exact_dot(partial_basis, exact_dot(partial_basis.T, column))
        column = column - exact_dot(partial_basis, exact_dot(partial_basis.T, column))
        column = column / jnp.sqrt(jnp.sum(column * column))
        return lax.dynamic_update_slice_in_dim(partial_basis, column, column_index, 1)

    return lax.fori_loop(0, matrix.shape[1], column_step, jnp.zeros_like(matrix))


def select_matrix(chosen, total):
    return (jnp.arange(total)[:, None] == chosen[None, :]).astype(jnp.float32)


def small_step(lower_factor, lower_inverse_mat, cross_inverse, rayleigh, schur_order, kept_index):
    total = rayleigh.shape[0]
    turned = exact_dot(exact_dot(lower_factor.T, rayleigh), lower_inverse_mat.T)
    select_order = select_matrix(schur_order, total)
    permuted = exact_dot(exact_dot(select_order.T, turned), select_order)
    orthogonal = orthonormal(permuted)
    kept_basis = exact_dot(orthogonal, select_matrix(kept_index, total))
    restarted = exact_dot(exact_dot(kept_basis.T, permuted), kept_basis)
    return (
        restarted,
        exact_dot(kept_basis.T, lower_inverse_mat),
        exact_dot(kept_basis.T, cross_inverse),
    )


def laplace(vector_columns, rim_map, inverse_map):
    wrapped = padded_2(vector_columns, (("sector", 1),), 1, True)
    lower_rim = jnp.take(wrapped[:, 0], inverse_map, axis=2)
    upper_rim = jnp.take(wrapped[:, -1], rim_map, axis=2)
    forward = jnp.concatenate([vector_columns[:, 1:], upper_rim[:, None]], axis=1)
    behind = jnp.concatenate([lower_rim[:, None], vector_columns[:, :-1]], axis=1)
    slab_split = padded_2(vector_columns, (("slab", 2),), 1, False)
    padded = jnp.pad(vector_columns, ((0, 0), (0, 0), (0, 0), (1, 1)))
    final_result = 6.0 * vector_columns - forward - behind
    final_result = final_result - slab_split[:, :, 2:] - slab_split[:, :, :-2]
    return final_result - padded[..., 2:] - padded[..., :-2]


def local(right_basis, left_basis, speed_squared, rayleigh, schur_order, kept_index, rim_map):
    basis_count = right_basis.shape[0]
    kept_count = kept_index.shape[0]
    grid_shape = speed_squared.shape
    right_rows = right_basis.reshape(basis_count, -1)
    left_rows = left_basis.reshape(basis_count, -1)
    flat_speed = speed_squared.reshape(1, -1)
    radial_count = rim_map.shape[0]
    places = jnp.arange(radial_count, dtype=jnp.int32)
    inverse_map = jnp.sum(
        jnp.where(rim_map[:, None] == places[None, :], places[:, None], 0), axis=0
    )
    row_total = right_rows.shape[1] * lax.axis_size("sector") * lax.axis_size("slab")
    right_gram = lax.psum(exact_dot(right_rows, right_rows.T), ("sector", "slab")) / row_total
    lower_factor = jnp.linalg.cholesky(right_gram)
    lower_inverse_mat = lower_inverse(lower_factor)
    normalized = exact_dot(lower_inverse_mat, right_rows)
    cross_matrix = lax.psum(exact_dot(left_rows, normalized.T), ("sector", "slab")) / row_total
    cross_inverse = solve_inverse(cross_matrix)
    restarted, rotate_right, rotate_left = small_step(
        lower_factor, lower_inverse_mat, cross_inverse, rayleigh, schur_order, kept_index
    )
    new_right = exact_dot(rotate_right, right_rows)
    new_left = exact_dot(rotate_left, left_rows)
    stacked = jnp.concatenate([new_right, flat_speed * new_left], axis=0)
    applied = laplace(
        stacked.reshape((2 * kept_count,) + grid_shape), rim_map, inverse_map
    ).reshape(2 * kept_count, -1)
    right_image = flat_speed * applied[:kept_count] - new_right
    left_image = applied[kept_count:] - new_left
    out_shape = (kept_count,) + grid_shape
    return (
        new_right.reshape(out_shape),
        new_left.reshape(out_shape),
        right_image.reshape(out_shape),
        left_image.reshape(out_shape),
        restarted,
    )


def solution(mesh):
    return jax.shard_map(
        local,
        mesh=mesh,
        in_specs=(
            P(None, "sector", "slab", None),
            P(None, "sector", "slab", None),
            P("sector", "slab", None),
            P(),
            P(),
            P(),
            P(),
        ),
        out_specs=(
            P(None, "sector", "slab", None),
            P(None, "sector", "slab", None),
            P(None, "sector", "slab", None),
            P(None, "sector", "slab", None),
            P(),
        ),
        check_vma=False,
    )
```

profile of v0, /device:TPU:1, one launch (start us, length us, event | category | flops | bytes accessed | tf_op | source)
XLA Modules:
  0.0 506.3 jit_solution(3654096387858231448)
XLA Ops:
  0.7 12.4 %fusion.9 = f32[64,64]{0,1:T(8,128)S(1)} fusion(f32[64,8,12,256]{3,1,2,0:T(8,128)} %param.14), kind=kOutput, calls=%fused_computation.28 | convolution fusion | flops 1207959552 | bytes 6307840 | tf_op jit(solution)/shard_map/dot_general | solution.py:21
  13.1 6.1 %copy.67 = f32[64,8,12,256]{3,2,1,0:T(8,128)} copy(f32[64,8,12,256]{3,1,2,0:T(8,128)S(1)} %copy-done.4) | data formatting | bytes 12582912 | tf_op args[0]
  19.2 69.0 %psum.14 = f32[64,64]{0,1:T(8,128)S(1)} all-reduce(f32[64,64]{0,1:T(8,128)S(1)} %fusion.9), channel_id=1, replica_groups=mesh['sector'=16,'slab'=8] {'sector','slab'}, use_global_device_ids=true, to_apply=%region_0.1 | all-reduce | flops 4096 | bytes 32768 | tf_op jit(solution)/shard_map/psum | solution.py:96
  88.3 5.8 %cholesky.44 = f32[64,64]{1,0:T(8,128)S(1)} custom-call(f32[64,64]{1,0:T(8,128)S(1)} %fusion.21), custom_call_target="Cholesky" | custom-call | tf_op jit(solution)/shard_map/jit(cholesky)/cholesky | solution.py:97
  95.4 4.9 custom-call.10
  100.6 6.8 %reshape.80 = f32[64,24576]{1,0:T(8,128)} reshape(f32[64,8,12,256]{3,2,1,0:T(8,128)} %copy.67) | data formatting | bytes 12582912 | tf_op jit(solution)/shard_map/reshape | solution.py:87
  107.4 8.9 %copy.68 = f32[64,8,12,256]{3,2,1,0:T(8,128)} copy(f32[64,8,12,256]{3,1,2,0:T(8,128)} %param.15) | data formatting | bytes 12582912 | tf_op args[1]
  116.3 6.8 %reshape.82 = f32[64,24576]{1,0:T(8,128)} reshape(f32[64,8,12,256]{3,2,1,0:T(8,128)} %copy.68) | data formatting | bytes 12582912 | tf_op jit(solution)/shard_map/reshape | solution.py:88
  123.0 8.1 %fusion.50 = f32[64,24576]{1,0:T(8,128)S(1)} fusion(f32[64,64]{1,0:T(8,128)S(1)} %fusion.19, f32[64,24576]{1,0:T(8,128)} %reshape.80), kind=kOutput, calls=%fused_computation.89 | convolution fusion | flops 1207959552 | bytes 12599296 | tf_op jit(solution)/shard_map/dot_general | solution.py:21
  131.2 5.1 %convolution_bitcast_fusion.4 = f32[64,64]{0,1:T(8,128)S(1)} fusion(f32[64,24576]{1,0:T(8,128)S(1)} %fusion.50, f32[64,24576]{1,0:T(8,128)S(1)} %copy-done.2), kind=kOutput, calls=%fused_computation.29 | convolution fusion | flops 1207959552 | bytes 12599296 | tf_op jit(solution)/shard_map/dot_general | solution.py:21
  136.3 62.7 %psum.15 = f32[64,64]{0,1:T(8,128)S(1)} all-reduce(f32[64,64]{0,1:T(8,128)S(1)} %convolution_bitcast_fusion.4), channel_id=1, replica_groups=mesh['sector'=16,'slab'=8] {'sector','slab'}, use_global_device_ids=true, to_apply=%region_6.9 | all-reduce | flops 4096 | bytes 32768 | tf_op jit(solution)/shard_map/psum | solution.py:100
  199.2 5.8 %cholesky.55 = f32[64,64]{1,0:T(8,128)S(1)} custom-call(f32[64,64]{1,0:T(8,128)S(1)} %fusion.18), custom_call_target="Cholesky" | custom-call | tf_op jit(solution)/shard_map/jit(cholesky)/cholesky | solution.py:31
  206.4 4.9 custom-call.8
  213.3 128.1 %while.13 = (s32[]{:T(128)}, f32[64,64]{0,1:T(8,128)S(1)}, f32[64,64]{0,1:T(8,128)S(1)}, s32[]{:T(128)}, s32[]{:T(128)}) while((s32[]{:T(128)}, f32[64,64]{0,1:T(8,128)S(1)}, f32[64,64]{0,1:T(8,128)S(1)}, s32[]{:T(128)}, s32[]{:T(128)}) %tuple.51), condition=%wide.region_5.0_spmd, body=%wide.region_3.0_spmd.sunk | while | flops 196929 | bytes 85849 | solution.py:48
  342.0 5.3 %fusion.49 = f32[32,24576]{1,0:T(8,128)S(1)} fusion(f32[32,64]{1,0:T(8,128)S(1)} %fusion.48, f32[64,24576]{1,0:T(8,128)} %reshape.80), kind=kOutput, calls=%fused_computation.88 | convolution fusion | flops 603979776 | bytes 9445376 | tf_op jit(solution)/shard_map/dot_general | solution.py:21
  347.3 4.9 broadcast_multiply_fusion
  352.2 3.1 pad_maximum_fusion.2
  355.4 7.0 %reshape.84 = f32[64,8,12,256]{3,2,1,0:T(8,128)} reshape(f32[64,24576]{1,0:T(8,128)} %pad_maximum_fusion.2) | data formatting | bytes 12582912 | tf_op jit(solution)/shard_map/reshape | solution.py:109
  362.4 1.7 fusion.44
  364.1 1.3 copy.74
  365.4 1.9 collective-permute-start.1
  367.3 1.3 copy.71
  368.9 5.5 %fusion.46 = (f32[64,8,1,256]{3,2,1,0:T(1,128)}, f32[64,8,1,256]{3,2,1,0:T(1,128)}) fusion(f32[64,8,12,256]{3,2,1,0:T(8,128)} %reshape.84), kind=kLoop, calls=%fused_computation.85 | loop fusion | bytes 2097152 | tf_op jit(solution)/shard_map/slice | solution.py:13
  374.4 1.3 collective-permute-start.2
  375.7 6.3 %collective-permute-start.3 = (f32[64,8,1,256]{3,2,1,0:T(1,128)}, f32[64,8,1,256]{3,2,1,0:T(1,128)}, u32[]{:S(2)}, u32[]{:S(2)}) collective-permute-start(f32[64,8,1,256]{3,2,1,0:T(1,128)} %get-tuple-element.120), channel_id=1, source_target_pairs={{0,1},{1,2},{2,3},{3,4},{4,5},{5,6},{6,7},{8,9},{9,10},{10,11},{11... | collective-permute-start | bytes 1572872 | tf_op jit(solution)/shard_map/ppermute | solution.py:14
  382.0 12.2 %fusion.45 = (f32[64,7,12,256]{3,2,1,0:T(8,128)}, f32[64,7,12,256]{3,2,1,0:T(8,128)}) fusion(f32[64,8,12,256]{3,2,1,0:T(8,128)} %reshape.84), kind=kLoop, calls=%fused_computation.84 | loop fusion | bytes 22020096 | tf_op jit(solution)/shard_map/slice | solution.py:75
  394.4 2.5 reshape.81
  396.8 3.9 reshape.83
  400.7 6.9 %copy.78 = f32[32,8,12,256]{3,1,2,0:T(8,128)} copy(f32[32,8,12,256]{3,2,1,0:T(8,128)} %reshape.83) | data formatting | bytes 6291456
  407.6 4.5 copy.77
  413.0 3.6 copy.75
  416.6 3.7 gather_fusion.1
  420.3 3.2 select_bitcast_fusion
  423.6 3.9 copy.76
  427.4 3.6 copy.72
  431.0 3.7 gather_fusion
  434.7 3.2 select_bitcast_fusion.1
  438.0 3.8 copy.73
  441.8 23.0 %fusion.3 = f32[64,8,12,256]{3,2,1,0:T(8,128)S(1)} fusion(f32[64,8,12,256]{3,2,1,0:T(8,128)} %reshape.84, f32[64,8,1,256]{3,2,1,0:T(1,128)} %collective-permute-done.3, f32[64,8,1,256]{3,2,1,0:T(1,128)} %collective-permute-done.2, f32[64,1,12,256]{3,2,1,0:T(8,128)} %copy.73, f32[64,7,12,256]{3,2,1,0:T(8,128)} %get-tuple-element.118, ...), kind=kLoop, calls=%fused_computation.14 | loop fusion | flops 17301504 | bytes 26214400 | tf_op jit(solution)/shard_map/sub | solution.py:80
  464.8 4.2 fusion.43
  469.0 3.7 slice.67
  472.7 4.8 sub.45
  477.5 3.8 reshape.86
  481.3 6.7 %copy.80 = f32[32,8,12,256]{3,1,2,0:T(8,128)} copy(f32[32,8,12,256]{3,2,1,0:T(8,128)} %reshape.86) | data formatting | bytes 6291456
  488.0 3.7 slice.65
  491.7 3.9 multiply_subtract_fusion
  495.6 3.7 reshape.85
  499.3 6.7 %copy.79 = f32[32,8,12,256]{3,1,2,0:T(8,128)} copy(f32[32,8,12,256]{3,2,1,0:T(8,128)} %reshape.85) | data formatting | bytes 6291456
  (444 shorter events, 89.2 us)
Async XLA Ops:
  0.6 211.1 %copy-start = (f32[64,64]{1,0:T(8,128)S(1)}, f32[64,64]{1,0:T(8,128)}, u32[]{:S(2)}) copy-start(f32[64,64]{1,0:T(8,128)} %param.17) | copy-start | bytes 49156
  0.6 12.4 %copy-start.4 = (f32[64,8,12,256]{3,1,2,0:T(8,128)S(1)}, f32[64,8,12,256]{3,1,2,0:T(8,128)}, u32[]{:S(2)}) copy-start(f32[64,8,12,256]{3,1,2,0:T(8,128)} %param.14) | copy-start | bytes 18874372
  123.0 8.1 %copy-start.2 = (f32[64,24576]{1,0:T(8,128)S(1)}, f32[64,24576]{1,0:T(8,128)}, u32[]{:S(2)}) copy-start(f32[64,24576]{1,0:T(8,128)} %reshape.82) | copy-start | bytes 18874372
  131.1 81.7 %copy-start.8 = (s32[64]{0:T(128)S(1)}, s32[64]{0:T(128)}, u32[]{:S(2)}) copy-start(s32[64]{0:T(128)} %param.18) | copy-start | bytes 772
  131.2 210.2 %copy-start.9 = (s32[32]{0:T(128)S(1)}, s32[32]{0:T(128)}, u32[]{:S(2)}) copy-start(s32[32]{0:T(128)} %param.19) | copy-start | bytes 388
  131.2 210.8 %copy-start.6 = (f32[8,12,256]{2,0,1:T(8,128)S(1)}, f32[8,12,256]{2,0,1:T(8,128)}, u32[]{:S(2)}) copy-start(f32[8,12,256]{2,0,1:T(8,128)} %param.16) | copy-start | bytes 294916
  342.0 5.3 %copy-start.3 = (f32[64,24576]{1,0:T(8,128)S(1)}, f32[64,24576]{1,0:T(8,128)}, u32[]{:S(2)}) copy-start(f32[64,24576]{1,0:T(8,128)} %reshape.82) | copy-start | bytes 18874372
  365.4 47.6 %collective-permute-start.1 = (f32[64,1,12,256]{3,0,2,1:T(8,128)}, f32[64,1,12,256]{3,0,2,1:T(8,128)}, u32[]{:S(2)}, u32[]{:S(2)}) collective-permute-start(f32[64,1,12,256]{3,0,2,1:T(8,128)} %copy.74), channel_id=1, source_target_pairs={{0,8},{8,16},{16,24},{24,32},{32,40},{40,48},{48,56},{56,64},{64,7... | collective-permute-start | bytes 2359304 | tf_op jit(solution)/shard_map/ppermute | solution.py:14
  368.7 58.7 %collective-permute-start = (f32[64,1,12,256]{3,0,2,1:T(8,128)}, f32[64,1,12,256]{3,0,2,1:T(8,128)}, u32[]{:S(2)}, u32[]{:S(2)}) collective-permute-start(f32[64,1,12,256]{3,0,2,1:T(8,128)} %copy.71), channel_id=1, source_target_pairs={{8,0},{16,8},{24,16},{32,24},{40,32},{48,40},{56,48},{64,56},{72,6... | collective-permute-start | bytes 2359304 | tf_op jit(solution)/shard_map/ppermute | solution.py:15
  374.4 67.4 %collective-permute-start.2 = (f32[64,8,1,256]{3,2,1,0:T(1,128)}, f32[64,8,1,256]{3,2,1,0:T(1,128)}, u32[]{:S(2)}, u32[]{:S(2)}) collective-permute-start(f32[64,8,1,256]{3,2,1,0:T(1,128)} %get-tuple-element.119), channel_id=1, source_target_pairs={{1,0},{2,1},{3,2},{4,3},{5,4},{6,5},{7,6},{9,8},{10,9},{11,10},{12... | collective-permute-start | bytes 1572872 | tf_op jit(solution)/shard_map/ppermute | solution.py:15
  375.7 18.5 %copy-start.7 = (s32[256]{0:T(256)S(1)}, s32[256]{0:T(256)}, u32[]{:S(2)}) copy-start(s32[256]{0:T(256)} %param.20) | copy-start | bytes 3076
  375.7 66.1 %collective-permute-start.3 = (f32[64,8,1,256]{3,2,1,0:T(1,128)}, f32[64,8,1,256]{3,2,1,0:T(1,128)}, u32[]{:S(2)}, u32[]{:S(2)}) collective-permute-start(f32[64,8,1,256]{3,2,1,0:T(1,128)} %get-tuple-element.120), channel_id=1, source_target_pairs={{0,1},{1,2},{2,3},{3,4},{4,5},{5,6},{6,7},{8,9},{9,10},{10,11},{11... | collective-permute-start | bytes 1572872 | tf_op jit(solution)/shard_map/ppermute | solution.py:14
  400.7 6.9 %copy-start.5 = (f32[32,8,12,256]{3,2,1,0:T(8,128)S(1)}, f32[32,8,12,256]{3,2,1,0:T(8,128)}, u32[]{:S(2)}) copy-start(f32[32,8,12,256]{3,2,1,0:T(8,128)} %reshape.81) | copy-start | bytes 9437188
  491.7 14.4 %copy-start.1 = (f32[64,64]{1,0:T(8,128)S(1)}, f32[64,64]{1,0:T(8,128)}, u32[]{:S(2)}) copy-start(f32[64,64]{1,0:T(8,128)} %param.17) | copy-start | bytes 49156
where the time goes:
time: 514 us; the launch traced here: 506 us
  local copies, waits for them, and re-layouts  133 us (26%)
  blocking collectives  132 us (26%)
  matrix products  119 us (23%)
  other arithmetic  66 us (13%)
  loops' own time  45.8 us (9%)
  starting transfers between devices  9.64 us (2%)
    dot_general x271, matrix products, exact_dot(): jnp.dot(left_operator, right_operator, precision=lax.Precision.HIGHEST)  118 us
    psum x1, blocking collectives, local(): lax.psum(exact_dot(right_rows, right_rows.T), ('sector', 'slab'))  69 us
    psum x1, blocking collectives, local(): lax.psum(exact_dot(left_rows, normalized.T), ('sector', 'slab')) / row_total  62.7 us
    another operation x1, loops' own time, orthonormal(): lax.fori_loop(0, matrix.shape[1], column_step, jnp.zeros_like(matrix))  45.8 us
    unnamed x27, local copies, waits for them, and re-layouts  39.8 us
    sub x1, other arithmetic, laplace(): return final_result - padded[..., 2:] - padded[..., :-2]  23 us
    slice x1, local copies, waits for them, and re-layouts, laplace(): vector_columns[:, :-1]  12.2 us
  transfers between devices with their start and end apart: 4, of which 0 were waited for; matrix products, arithmetic and copies ran while one was open for 13% of the time, Pallas kernels for 0%

commit v1 on v0

v1 whole, which is shorter than its diff:
```python
import jax
import jax.numpy as jnp
from jax import lax
from jax.experimental import pallas as pl
from jax.experimental.pallas import tpu as pltpu
from jax.sharding import PartitionSpec as P

MESH = pl.DeviceIdType.MESH
NN = (((1,), (0,)), ((), ()))
NT = (((1,), (1,)), ((), ()))
TN = (((0,), (0,)), ((), ()))
F32 = jnp.float32
BF16 = jnp.bfloat16
K, KEEP, CT, CA, CR = 64, 32, 8, 12, 256
CELLS = 3145728


def mm(a, b, dims=NN):
    return lax.dot_general(a, b, dims, precision=lax.Precision.HIGHEST, preferred_element_type=F32)


def mm16(a, b, dims=NN):
    return lax.dot_general(a, b, dims, preferred_element_type=F32)


def iota(shape, dim):
    return lax.broadcasted_iota(jnp.int32, shape, dim)


def split(x):
    high = x.astype(BF16)
    return high, (x - high.astype(F32)).astype(BF16)


def stacked(right, left):
    return jnp.concatenate(split(right) + split(left), axis=0)


def halves(pair):
    return jnp.concatenate(pair, axis=1)


def gram_kernel(right_ref, left_ref, speed_ref, rim_ref, part_ref, cells_ref, ang_ref, ax_ref, buf_ref, sem):
    refs = (right_ref, left_ref)

    @pl.loop(0, CA)
    def _(a):
        for n in range(2):
            for t in range(CT):
                for j in range(2):
                    pltpu.make_async_copy(refs[n].at[:, a, j, t, :], buf_ref.at[a, n, t, j], sem.at[a]).start()

    part_ref[...] = jnp.zeros_like(part_ref)
    hot = (iota((CR, CR), 0) == rim_ref[...]).astype(BF16)

    def scaled(a, t):
        fields = []
        for j in range(2):
            fields.append(speed_ref[a, j, t:t + 1, :] * buf_ref[a, 1, t, j])
        return split(halves(fields))

    def axial(side, a):
        for t in range(CT):
            plain = cells_ref[a, 0:128, t * CR:(t + 1) * CR]
            ax_ref[side, t] = jnp.concatenate((plain,) + scaled(a, t), axis=0)

    @pl.loop(0, CA)
    def _(a):
        pltpu.make_async_copy(buf_ref.at[a], buf_ref.at[a], sem.at[a]).wait()
        columns = []
        for t in range(CT):
            for j in range(2):
                columns.append(stacked(buf_ref[a, 0, t, j], buf_ref[a, 1, t, j]))
        x = halves(columns)
        cells_ref[a] = x
        part_ref[...] += mm16(x[:128], x, NT)
        for side, t in ((0, 0), (1, CT - 1)):
            edge = jnp.concatenate((x[:128, t * CR:(t + 1) * CR],) + scaled(a, t), axis=0)
            ang_ref[side, a] = mm16(edge, hot, NT if side else NN).astype(BF16)

        @pl.when(a == 0)
        def _():
            axial(0, a)

        @pl.when(a == CA - 1)
        def _():
            axial(1, a)


def gram(right, left, speed, rim):
    vmem = pl.BlockSpec(memory_space=pltpu.VMEM)
    main = pl.BlockSpec(memory_space=pltpu.HBM)
    return pl.pallas_call(
        gram_kernel,
        in_specs=[main, main, vmem, vmem],
        out_specs=[vmem] * 4,
        out_shape=[
            jax.ShapeDtypeStruct((128, 256), F32),
            pltpu.VMEM((CA, 256, CT * CR), BF16),
            jax.ShapeDtypeStruct((2, CA, 256, CR), BF16),
            jax.ShapeDtypeStruct((2, CT, 256, CR), BF16),
        ],
        scratch_shapes=[pltpu.VMEM((CA, 2, CT, 2, 64, 128), F32), pltpu.SemaphoreType.DMA((CA,))],
        compiler_params=pltpu.CompilerParams(vmem_limit_bytes=20 << 20),
        name="gram",
    )(pltpu.with_memory_space_constraint(right, pltpu.HBM), pltpu.with_memory_space_constraint(left, pltpu.HBM), speed, rim)


def place(sector, slab):
    return sector // 4, slab // 2, (slab % 2) * 2 + (sector // 2) % 2, sector % 2


def device(x, y, z, core):
    return (x * 4 + (z % 2) * 2 + core, y * 2 + z // 2)


def combined(part):
    top = part[:64] + part[64:]
    gram, cross = top[:, :128], top[:, 128:]
    gram, cross = gram + pltpu.roll(gram, 64, 1), cross + pltpu.roll(cross, 64, 1)
    return jnp.where(iota((64, 128), 1) < 64, gram, cross)


def reduce_kernel(raw_ref, out_ref, part_ref, got_ref, send_sem, recv_sem):
    part_ref[...] = combined(raw_ref[...])
    x, y, z, core = place(lax.axis_index("sector"), lax.axis_index("slab"))
    other = device(x, y, z, 1 - core)
    groups = (
        (x, [device(lax.rem(x + o, 4), y, z, core) for o in (1, 2, 3)]),
        (y, [device(x, lax.rem(y + o, 4), z, core) for o in (1, 2, 3)]),
        (z, [device(x, y, lax.rem(z + o, 4), core) for o in (1, 2, 3)]),
    )
    barrier = pltpu.get_barrier_semaphore()
    for peer in [other] + [p for _, peers in groups for p in peers]:
        pl.semaphore_signal(barrier, inc=1, device_id=peer, device_id_type=MESH)
    pl.semaphore_wait(barrier, 10)

    def send(src, dst, n, peer):
        copy = pltpu.make_async_remote_copy(
            src_ref=src, dst_ref=dst, send_sem=send_sem.at[n], recv_sem=recv_sem.at[n],
            device_id=peer, device_id_type=MESH)
        copy.start()
        return copy

    def half(h):
        return pl.ds(pl.multiple_of(h * 32, 32), 32)

    copies = [send(part_ref.at[half(1 - core)], got_ref.at[0, 0], 0, other)]
    copies[0].wait_recv()
    mine, theirs = part_ref[half(core), :], got_ref[0, 0]
    total = mine + theirs
    n = 1
    for stage, (me, peers) in enumerate(groups):
        got_ref[stage + 1, me] = total
        sent = []
        for peer in peers:
            sent.append(send(got_ref.at[stage + 1, me], got_ref.at[stage + 1, me], n, peer))
            n += 1
        for copy in sent:
            copy.wait_recv()
        copies += sent
        total = (got_ref[stage + 1, 0] + got_ref[stage + 1, 1]) + (got_ref[stage + 1, 2] + got_ref[stage + 1, 3])
    out_ref[half(core), :] = total
    copies.append(send(out_ref.at[half(core)], out_ref.at[half(core)], n, other))
    copies[-1].wait_recv()
    for copy in copies:
        copy.wait_send()


def reduced(part):
    vmem = pl.BlockSpec(memory_space=pltpu.VMEM)
    return pl.pallas_call(
        reduce_kernel,
        in_specs=[vmem],
        out_specs=vmem,
        out_shape=jax.ShapeDtypeStruct((64, 128), F32),
        scratch_shapes=[pltpu.VMEM((64, 128), F32), pltpu.VMEM((4, 4, 32, 128), F32), pltpu.SemaphoreType.DMA((11,)), pltpu.SemaphoreType.DMA((11,))],
        compiler_params=pltpu.CompilerParams(collective_id=0, has_side_effects=True, vmem_limit_bytes=4 << 20),
        name="reduced",
    )(part)


def pivot(a, k, rows):
    scaled = a[k:k + 1, :] * (1.0 / a[k:k + 1, k:k + 1])
    return a - jnp.where(rows > k, a[:, k:k + 1], 0.0) * scaled


def unit_rows(a, eye):
    return a * lax.rsqrt(jnp.sum(a[:, :64] * eye, axis=1, keepdims=True))


def small_step(gc, rayleigh, order, kept):
    rows = iota((64, 1), 0)
    r64, c64 = iota((64, 64), 0), iota((64, 64), 1)
    eye = (r64 == c64).astype(F32)
    order_col = jnp.sum(jnp.where(r64 == c64, order, 0).astype(F32), axis=1, keepdims=True).astype(jnp.int32)
    kept_col = jnp.sum(jnp.where(iota((32, 32), 0) == iota((32, 32), 1), kept, 0).astype(F32), axis=1, keepdims=True).astype(jnp.int32)
    select_order = (order_col == c64).astype(F32)
    select_kept = (kept_col == iota((32, 64), 1)).astype(F32)
    cross_t = gc[:, 64:]
    a1 = jnp.concatenate([gc[:, :64], eye], axis=1)
    a2 = jnp.concatenate([mm(cross_t, cross_t, NT), eye], axis=1)
    for k in range(64):
        a1 = pivot(a1, k, rows)
        a2 = pivot(a2, k, rows)
    a1, a2 = unit_rows(a1, eye), unit_rows(a2, eye)
    lower_t, lower_inv, cross_low = a1[:, :64], a1[:, 64:], a2[:, 64:]
    side = mm(lower_inv, rayleigh, NT)
    ordered = mm(select_order, jnp.concatenate([lower_t, side], axis=1))
    permuted_t = mm(ordered[:, 64:], ordered[:, :64], NT)
    a3 = jnp.concatenate([mm(permuted_t, permuted_t, NT), permuted_t], axis=1)
    cross_inv = mm(cross_low, mm(cross_low, cross_t), TN)
    cross_inv = cross_inv + mm(cross_inv, eye - mm(cross_t, cross_inv, TN))
    tail = jnp.concatenate([lower_inv, mm(lower_t, cross_inv)], axis=1)
    for k in range(64):
        a3 = pivot(a3, k, rows)
    basis_t = unit_rows(a3, eye)[:, 64:]
    weight = jnp.where(r64 > c64, 1.0, jnp.where(r64 == c64, 0.5, 0.0))
    for _ in range(2):
        basis_t = basis_t - mm((mm(basis_t, basis_t, NT) - eye) * weight, basis_t)
    kept_t = mm(select_kept, basis_t)
    restarted = mm(mm(kept_t, permuted_t, NT), kept_t, NT)
    return mm(kept_t, tail), restarted


def rotation_blocks(rotation):
    high, low = split(rotation)
    zero = jnp.zeros((KEEP, 128), BF16)

    def both(part):
        right, left = part[:, :64], part[:, 64:]
        return [
            jnp.concatenate([right, right, zero], axis=1),
            jnp.concatenate([zero, left, left], axis=1),
        ]

    return jnp.concatenate(both(high) + both(low), axis=0)


def small_kernel(gc_ref, rayleigh_ref, order_ref, kept_ref, rotate_ref, restarted_ref):
    rotation, restarted = small_step(gc_ref[...] * (1.0 / CELLS), rayleigh_ref[...], order_ref[...], kept_ref[...])
    rotate_ref[...] = rotation_blocks(rotation)
    restarted_ref[...] = restarted


def small(gc, rayleigh, order, kept):
    vmem = pl.BlockSpec(memory_space=pltpu.VMEM)
    return pl.pallas_call(
        small_kernel,
        in_specs=[vmem] * 4,
        out_specs=[vmem] * 2,
        out_shape=[jax.ShapeDtypeStruct((128, 256), BF16), jax.ShapeDtypeStruct((KEEP, KEEP), F32)],
        compiler_params=pltpu.CompilerParams(vmem_limit_bytes=6 << 20),
        name="small",
    )(gc, rayleigh, order, kept)


def rotated(rotate, block):
    both = mm16(rotate, block)
    return both[:64] + both[64:]


def halo_kernel(rotate_ref, ang_ref, ax_ref, ang_out, ax_out, ang_buf, ax_buf, send_sem, recv_sem):
    sector, slab = lax.axis_index("sector"), lax.axis_index("slab")
    targets = (
        (lax.rem(sector + 15, 16), slab),
        (lax.rem(sector + 1, 16), slab),
        (sector, lax.rem(slab + 7, 8)),
        (sector, lax.rem(slab + 1, 8)),
    )
    barrier = pltpu.get_barrier_semaphore()
    for target in targets:
        pl.semaphore_signal(barrier, inc=1, device_id=target, device_id_type=MESH)
    rotate = rotate_ref[...]
    copies = []
    for n, target in enumerate(targets):
        buf, out = ((ang_buf, ang_out), (ax_buf, ax_out))[n // 2]
        side = n % 2
        copies.append(pltpu.make_async_remote_copy(
            src_ref=buf.at[side], dst_ref=out.at[1 - side], send_sem=send_sem.at[n], recv_sem=recv_sem.at[n],
            device_id=target, device_id_type=MESH))

    def fill(n):
        buf, ref = ((ang_buf, ang_ref), (ax_buf, ax_ref))[n // 2]
        side = n % 2

        @pl.loop(0, buf.shape[1])
        def _(i):
            buf[side, i] = rotated(rotate, ref[side, i])

    fill(2)
    pl.semaphore_wait(barrier, 4)

    @pl.when(slab > 0)
    def _():
        copies[2].start()

    fill(3)

    @pl.when(slab < 7)
    def _():
        copies[3].start()

    fill(0)
    copies[0].start()
    fill(1)
    copies[1].start()
    copies[0].wait()
    copies[1].wait()

    @pl.when(slab > 0)
    def _():
        copies[2].wait_send()
        copies[3].wait_recv()

    @pl.when(slab < 7)
    def _():
        copies[3].wait_send()
        copies[2].wait_recv()


def halos(rotate, ang, ax):
    vmem = pl.BlockSpec(memory_space=pltpu.VMEM)
    anywhere = pl.BlockSpec(memory_space=pl.ANY)
    return pl.pallas_call(
        halo_kernel,
        in_specs=[vmem] * 3,
        out_specs=[anywhere] * 2,
        out_shape=[jax.ShapeDtypeStruct((2, CA, 64, CR), F32), jax.ShapeDtypeStruct((2, CT, 64, CR), F32)],
        scratch_shapes=[pltpu.VMEM((2, CA, 64, CR), F32), pltpu.VMEM((2, CT, 64, CR), F32),
                        pltpu.SemaphoreType.DMA((4,)), pltpu.SemaphoreType.DMA((4,))],
        compiler_params=pltpu.CompilerParams(collective_id=1, has_side_effects=True, vmem_limit_bytes=8 << 20),
        name="halos",
    )(rotate, ang, ax)


def image_kernel(rotate_ref, cells_ref, speed_ref, ang_ref, ax_ref, new_right_ref, new_left_ref, right_image_ref,
                 left_image_ref, field_ref, plain_ref, image_ref, sem):
    slab = lax.axis_index("slab")
    outs = (new_right_ref, new_left_ref, right_image_ref, left_image_ref)
    rotate = rotate_ref[...]
    zero = jnp.zeros((64, 128), F32)

    @pl.loop(0, CT)
    def _(t):
        for j in range(2):
            field_ref[0, t, j] = jnp.where(slab > 0, ax_ref[0, t, :, j * 128:(j + 1) * 128], zero)
            field_ref[CA + 1, t, j] = jnp.where(slab < 7, ax_ref[1, t, :, j * 128:(j + 1) * 128], zero)

    def send(n, src, a, t, j):
        pltpu.make_async_copy(src, outs[n].at[:, a, j, t, :], sem.at[n]).start()

    @pl.loop(0, CA + 1)
    def _(step):
        @pl.when(step < CA)
        def _():
            a = step
            for t in range(CT):
                value = rotated(rotate, cells_ref[a, :, t * CR:(t + 1) * CR])
                for j in range(2):
                    part = value[:, j * 128:(j + 1) * 128]
                    field_ref[a + 1, t, j, 0:KEEP] = part[:KEEP]
                    field_ref[a + 1, t, j, KEEP:] = part[KEEP:] * speed_ref[a, j, t:t + 1, :]
                    plain_ref[a, t, j] = part[KEEP:]
            for t in range(CT):
                for j in range(2):
                    send(0, field_ref.at[a + 1, t, j, 0:KEEP], a, t, j)
                    send(1, plain_ref.at[a, t, j], a, t, j)

        @pl.when(step > 0)
        def _():
            a = step - 1
            lanes = iota((64, 128), 1)
            for t in range(CT):
                mid = [field_ref[a + 1, t, j] for j in range(2)]
                up = [pltpu.roll(m, 1, 1) for m in mid]
                down = [pltpu.roll(m, 127, 1) for m in mid]
                behind = [jnp.where(lanes == 0, 0.0, up[0]), jnp.where(lanes == 0, up[0], up[1])]
                ahead = [jnp.where(lanes == 127, down[1], down[0]), jnp.where(lanes == 127, 0.0, down[1])]
                for j in range(2):
                    total = field_ref[a, t, j] + field_ref[a + 2, t, j]
                    total = total + (field_ref[a + 1, t - 1, j] if t > 0 else ang_ref[0, a, :, j * 128:(j + 1) * 128])
                    total = total + (field_ref[a + 1, t + 1, j] if t < CT - 1 else ang_ref[1, a, :, j * 128:(j + 1) * 128])
                    applied = 6.0 * mid[j] - total - behind[j] - ahead[j]
                    image_ref[a, t, j, 0:KEEP] = applied[:KEEP] * speed_ref[a, j, t:t + 1, :] - mid[j][:KEEP]
                    image_ref[a, t, j, KEEP:] = applied[KEEP:] - plain_ref[a, t, j]
            for t in range(CT):
                for j in range(2):
                    send(2, image_ref.at[a, t, j, 0:KEEP], a, t, j)
                    send(3, image_ref.at[a, t, j, KEEP:], a, t, j)

    for n in range(4):
        pltpu.make_async_copy(outs[n], outs[n], sem.at[n]).wait()


def images(rotate, cells, speed, ang, ax):
    vmem = pl.BlockSpec(memory_space=pltpu.VMEM)
    main = pl.BlockSpec(memory_space=pltpu.HBM)
    kept = jax.ShapeDtypeStruct((KEEP, CA, 2, CT, 128), F32)
    return pl.pallas_call(
        image_kernel,
        in_specs=[vmem] * 5,
        out_specs=[main] * 4,
        out_shape=[kept] * 4,
        scratch_shapes=[pltpu.VMEM((CA + 2, CT, 2, 64, 128), F32), pltpu.VMEM((CA, CT, 2, KEEP, 128), F32),
                        pltpu.VMEM((CA, CT, 2, 64, 128), F32), pltpu.SemaphoreType.DMA((4,))],
        compiler_params=pltpu.CompilerParams(vmem_limit_bytes=22 << 20),
        name="images",
    )(rotate, pltpu.with_memory_space_constraint(cells, pltpu.VMEM), speed, ang, ax)


def tiles(array):
    return array.reshape(array.shape[0], CT, CA, 2, 128).transpose(0, 2, 3, 1, 4)


def local(right_basis, left_basis, speed_squared, rayleigh, schur_order, kept_index, rim_map):
    right, left, speed = tiles(right_basis), tiles(left_basis), tiles(speed_squared[None])[0]
    part, cells, ang, ax = gram(right, left, speed, rim_map.reshape(1, CR))
    rotate, restarted = small(reduced(part), rayleigh, schur_order.reshape(1, K), kept_index.reshape(1, KEEP))
    ang_halo, ax_halo = halos(rotate, ang, ax)
    outs = images(rotate, cells, speed, ang_halo, ax_halo)
    shape = (KEEP, CT, CA, CR)
    return tuple(o.transpose(0, 3, 1, 2, 4).reshape(shape) for o in outs) + (restarted,)


def solution(mesh):
    fields = P(None, "sector", "slab", None)
    return jax.shard_map(
        local,
        mesh=mesh,
        in_specs=(fields, fields, P("sector", "slab", None), P(), P(), P(), P()),
        out_specs=(fields, fields, fields, fields, P()),
        check_vma=False,
    )
```

time: 514 us -> 99.2 us (0.19); the launches traced: 506 us -> 99 us
  blocking collectives: 132 us -> 0 us
  local copies, waits for them, and re-layouts: 133 us -> 1.58 us
  matrix products: 119 us -> 0 us
  Pallas kernels: 0 us -> 96.7 us
  other arithmetic: 66 us -> 0 us
  loops' own time: 45.8 us -> 0 us
  starting transfers between devices: 9.64 us -> 0 us
    psum x2 -> x0, blocking collectives: 132 us -> none  [the longest x1 69 us: local(): lax.psum(exact_dot(right_rows, right_rows.T), ('sector', 'slab'))]
    dot_general x271 -> x0, matrix products: 118 us -> none  [exact_dot(): jnp.dot(left_operator, right_operator, precision=lax.Precision.HIGHEST)]
    pallas_call x0 -> x5, Pallas kernels: none -> 96.7 us  [the longest x1 43.4 us: halos(): pl.pallas_call(halo_kernel, in_specs=[vmem] * 3, out_specs=[anywhere] * 2...]
    another operation x1 -> x0, loops' own time: 45.8 us -> none  [orthonormal(): lax.fori_loop(0, matrix.shape[1], column_step, jnp.zeros_like(matrix))]
    unnamed x27 -> x12, local copies, waits for them, and re-layouts: 39.8 us -> 1.58 us
    reshape x7 -> x0, local copies, waits for them, and re-layouts: 34.4 us -> none  [the longest x1 7.01 us: local(): stacked.reshape((2 * kept_count,) + grid_shape)]
    slice x8 -> x0, local copies, waits for them, and re-layouts: 33.7 us -> none  [the longest x1 12.2 us: laplace(): vector_columns[:, :-1]]
    sub x3 -> x0, other arithmetic: 31.8 us -> none  [the longest x1 23 us: laplace(): return final_result - padded[..., 2:] - padded[..., :-2]]
  transfers between devices with their start and end apart: 4 -> 0, of which waited for: 0 -> 0; matrix products, arithmetic and copies ran while one was open for 13% -> 0% of each run, Pallas kernels for 0% -> 0%
where the time goes in v1:
time: 99.2 us; the launch traced here: 99 us
  Pallas kernels  96.7 us (97%)
  local copies, waits for them, and re-layouts  1.58 us (2%)
    pallas_call x1, Pallas kernels, halos(): pl.pallas_call(halo_kernel, in_specs=[vmem] * 3, out_specs=[anywhere] * 2...  43.4 us
    pallas_call x1, Pallas kernels, reduced(): pl.pallas_call(reduce_kernel, in_specs=[vmem], out_specs=vmem, out_shape=...  20.3 us
    pallas_call x1, Pallas kernels, small(): pl.pallas_call(small_kernel, in_specs=[vmem] * 4, out_specs=[vmem] * 2, o...  14.7 us
    pallas_call x1, Pallas kernels, images(): pl.pallas_call(image_kernel, in_specs=[vmem] * 5, out_specs=[main] * 4, o...  9.73 us
    pallas_call x1, Pallas kernels, gram(): pl.pallas_call(gram_kernel, in_specs=[main, main, vmem, vmem], out_specs=...  8.52 us

profile of v1, /device:TPU:1, one launch (start us, length us, event | category | flops | bytes accessed | tf_op | source)
XLA Modules:
  0.0 99.0 jit_solution(15650526665422669902)
XLA Ops:
  0.6 0.0 copy-start
  0.6 0.9 copy-done
  1.5 0.0 copy-start.3
  1.5 0.7 copy-done.3
  2.2 0.0 copy-start.2
  2.2 0.0 copy-start.4
  2.2 0.0 copy-start.5
  2.2 8.5 %gram.1 = (f32[128,256]{1,0:T(8,128)S(1)}, bf16[12,256,2048]{2,1,0:T(8,128)(2,1)S(1)}, bf16[2,12,256,256]{3,2,1,0:T(8,128)(2,1)S(1)}, bf16[2,8,256,256]{3,2,1,0:T(8,128)(2,1)S(1)}) custom-call(f32[64,12,2,8,128]{4,3,2,1,0:T(8,128)} %bitcast.31, f32[64,12,2,8,128]{4,3,2,1,0:T(8,128)} %bitcast.32, f32[12,2,8,128]{3,2,1,0:T(8,128)S(1)} %bitcast.26, ...), custom_call_target="tpu_custom_call" | custom-call | tf_op jit(solution)/shard_map/gram/pallas_call | solution.py:93
  10.7 0.0 copy-start.1
  10.8 20.3 %reduced.1.gc_ref = f32[64,128]{1,0:T(8,128)S(1)} custom-call(f32[128,256]{1,0:T(8,128)S(1)} %get-tuple-element.17.raw_ref), custom_call_target="tpu_custom_call" | custom-call | tf_op jit(solution)/shard_map/reduced/pallas_call | solution.py:172
  31.1 0.0 copy-done.2
  31.1 0.0 copy-done.4
  31.1 0.0 copy-done.5
  31.1 14.7 %small.1 = (bf16[128,256]{1,0:T(8,128)(2,1)S(1)}, f32[32,32]{1,0:T(8,128)}) custom-call(f32[64,128]{1,0:T(8,128)S(1)} %reduced.1.gc_ref, f32[64,64]{1,0:T(8,128)S(1)} %copy-done.2, s32[1,64]{1,0:T(1,128)S(1)} %bitcast.29, s32[1,32]{1,0:T(1,128)S(1)} %bitcast.30), custom_call_target="tpu_custom_call" | custom-call | tf_op jit(solution)/shard_map/small/pallas_call | solution.py:248
  45.8 43.4 %halos.1 = (f32[2,12,64,256]{3,2,1,0:T(8,128)S(1)}, f32[2,8,64,256]{3,2,1,0:T(8,128)S(1)}) custom-call(bf16[128,256]{1,0:T(8,128)(2,1)S(1)} %get-tuple-element.18.rotate_ref, bf16[2,12,256,256]{3,2,1,0:T(8,128)(2,1)S(1)} %get-tuple-element.20.ang_ref, bf16[2,8,256,256]{3,2,1,0:T(8,128)(2,1)S(1)} %get-tuple-element.21.ax_ref), custom_call_target="tpu_custom_call" | custom-call | tf_op jit(solution)/shard_map/halos/pallas_call | solution.py:325
  89.3 0.0 copy-done.1
  89.3 9.7 %images.1 = (f32[32,12,2,8,128]{4,3,2,1,0:T(8,128)}, f32[32,12,2,8,128]{4,3,2,1,0:T(8,128)}, f32[32,12,2,8,128]{4,3,2,1,0:T(8,128)}, f32[32,12,2,8,128]{4,3,2,1,0:T(8,128)}) custom-call(bf16[128,256]{1,0:T(8,128)(2,1)S(1)} %get-tuple-element.18.rotate_ref, bf16[12,256,2048]{2,1,0:T(8,128)(2,1)S(1)} %get-tuple-element.19.cells_ref, ...), custom_call_target="tpu_custom_call" | custom-call | tf_op jit(solution)/shard_map/images/pallas_call | solution.py:400
Async XLA Ops:
  0.6 0.9 copy-start
  1.5 0.7 copy-start.3
  2.2 28.9 %copy-start.2 = (f32[64,64]{1,0:T(8,128)S(1)}, f32[64,64]{1,0:T(8,128)}, u32[]{:S(2)}) copy-start(f32[64,64]{1,0:T(8,128)} %rayleigh_ref.1) | copy-start | bytes 49156
  2.2 28.9 %copy-start.4 = (s32[64]{0:T(128)S(1)}, s32[64]{0:T(128)}, u32[]{:S(2)}) copy-start(s32[64]{0:T(128)} %param.11) | copy-start | bytes 772
  2.2 28.9 %copy-start.5 = (s32[32]{0:T(128)S(1)}, s32[32]{0:T(128)}, u32[]{:S(2)}) copy-start(s32[32]{0:T(128)} %param.12) | copy-start | bytes 388
  10.7 78.5 %copy-start.1 = (f32[8,12,256]{2,0,1:T(8,128)S(1)}, f32[8,12,256]{2,0,1:T(8,128)}, u32[]{:S(2)}) copy-start(f32[8,12,256]{2,0,1:T(8,128)} %param.9) | copy-start | bytes 294916

commit v2 on v0

v2 whole, which is shorter than its diff:
```python
import jax
import jax.numpy as jnp
from jax import lax
from jax.experimental import pallas as pl
from jax.experimental.pallas import tpu as pltpu
from jax.sharding import PartitionSpec as P

MESH = pl.DeviceIdType.MESH
NN = (((1,), (0,)), ((), ()))
NT = (((1,), (1,)), ((), ()))
TN = (((0,), (0,)), ((), ()))
F32 = jnp.float32
BF16 = jnp.bfloat16
K, KEEP, CT, CA, CR = 64, 32, 8, 12, 256
CELLS = 3145728
EARLY = 2
RAW = 4


def mm(a, b, dims=NN):
    return lax.dot_general(a, b, dims, precision=lax.Precision.HIGHEST, preferred_element_type=F32)


def mm16(a, b, dims=NN):
    return lax.dot_general(a, b, dims, preferred_element_type=F32)


def iota(shape, dim):
    return lax.broadcasted_iota(jnp.int32, shape, dim)


def split(x):
    high = x.astype(BF16)
    return high, (x - high.astype(F32)).astype(BF16)


def stacked(right, left):
    return jnp.concatenate(split(right) + split(left), axis=0)


def halves(pair):
    return jnp.concatenate(pair, axis=1)


def place(sector, slab):
    return sector // 4, slab // 2, (slab % 2) * 2 + (sector // 2) % 2, sector % 2


def device(x, y, z, core):
    return (x * 4 + (z % 2) * 2 + core, y * 2 + z // 2)


def combined(part):
    top = part[:64] + part[64:]
    gram, cross = top[:, :128], top[:, 128:]
    gram, cross = gram + pltpu.roll(gram, 64, 1), cross + pltpu.roll(cross, 64, 1)
    return jnp.where(iota((64, 128), 1) < 64, gram, cross)


def pivots(group, first):
    rows = iota((8, 128), 0)
    top = first // 8
    states = []
    for blocks in group:
        columns = [[jnp.broadcast_to(blocks[i][:, first + j:first + j + 1], (8, 128)) for i in range(top, 8)] for j in range(8)]
        corner = [[columns[j][0][i:i + 1, :] for j in range(8)] for i in range(8)]
        states.append((columns, corner, [blocks[top][i:i + 1, :] for i in range(8)], []))
    for j in range(8):
        for columns, corner, lead, scaled in states:
            inverse = 1.0 / corner[j][j]
            scaled.append(lead[j] * inverse)
            for m in range(j + 1, 8):
                factor = corner[m][j] * inverse
                for i in range(m, 8):
                    corner[i][m] = corner[i][m] - corner[i][j] * factor
                lead[m] = lead[m] - corner[m][j] * scaled[j]
                columns[m] = [c - d * factor for c, d in zip(columns[m], columns[j])]
    result = []
    for blocks, (columns, _, _, scaled) in zip(group, states):
        blocks = list(blocks)
        for i in range(top, 8):
            for j in range(8):
                column = columns[j][i - top]
                if i == top:
                    column = jnp.where(rows > j, column, 0.0)
                blocks[i] = blocks[i] - column * scaled[j]
        result.append(blocks)
    return result


def eliminate(arrays):
    rows, lanes = iota((8, 128), 0), iota((8, 128), 1)
    group = [[a[8 * i:8 * i + 8, :] for i in range(8)] for a in arrays]
    for first in range(0, 64, 8):
        group = pivots(group, first)
    result = []
    for blocks in group:
        scaled = []
        for i, block in enumerate(blocks):
            pivot = jnp.sum(jnp.where(lanes == rows + 8 * i, block, 0.0), axis=1, keepdims=True)
            scaled.append(block * lax.rsqrt(pivot))
        full = jnp.concatenate(scaled, axis=0)
        keep = jnp.logical_or(iota((64, 128), 1) >= 64, iota((64, 128), 1) >= iota((64, 128), 0))
        result.append(jnp.where(keep, full, 0.0))
    return result


def small_step(gc, rayleigh, order, kept):
    r64, c64 = iota((64, 64), 0), iota((64, 64), 1)
    eye = (r64 == c64).astype(F32)
    order_col = jnp.sum(jnp.where(r64 == c64, order, 0).astype(F32), axis=1, keepdims=True).astype(jnp.int32)
    kept_col = jnp.sum(jnp.where(iota((32, 32), 0) == iota((32, 32), 1), kept, 0).astype(F32), axis=1, keepdims=True).astype(jnp.int32)
    select_order = (order_col == c64).astype(F32)
    select_kept = (kept_col == iota((32, 64), 1)).astype(F32)
    cross_t = gc[:, 64:]
    a1 = jnp.concatenate([gc[:, :64], eye], axis=1)
    a2 = jnp.concatenate([mm(cross_t, cross_t, NT), eye], axis=1)
    a1, a2 = eliminate([a1, a2])
    lower_t, lower_inv, cross_low = a1[:, :64], a1[:, 64:], a2[:, 64:]
    side = mm(lower_inv, rayleigh, NT)
    ordered = mm(select_order, jnp.concatenate([lower_t, side], axis=1))
    permuted_t = mm(ordered[:, 64:], ordered[:, :64], NT)
    a3 = jnp.concatenate([mm(permuted_t, permuted_t, NT), permuted_t], axis=1)
    cross_inv = mm(cross_low, mm(cross_low, cross_t), TN)
    cross_inv = cross_inv + mm(cross_inv, eye - mm(cross_t, cross_inv, TN))
    tail = jnp.concatenate([lower_inv, mm(lower_t, cross_inv)], axis=1)
    basis_t = eliminate([a3])[0][:, 64:]
    weight = jnp.where(r64 > c64, 1.0, jnp.where(r64 == c64, 0.5, 0.0))
    for _ in range(2):
        basis_t = basis_t - mm((mm(basis_t, basis_t, NT) - eye) * weight, basis_t)
    kept_t = mm(select_kept, basis_t)
    restarted = mm(mm(kept_t, permuted_t, NT), kept_t, NT)
    return mm(kept_t, tail), restarted


def rotation_blocks(rotation):
    high, low = split(rotation)
    zero = jnp.zeros((KEEP, 128), BF16)

    def both(part):
        right, left = part[:, :64], part[:, 64:]
        return [
            jnp.concatenate([right, right, zero], axis=1),
            jnp.concatenate([zero, left, left], axis=1),
        ]

    return jnp.concatenate(both(high) + both(low), axis=0)


def rotated(rotate, block):
    both = mm16(rotate, block)
    return both[:64] + both[64:]


def core_kernel(right_ref, left_ref, speed_hbm, rim_hbm, rayleigh_hbm, order_hbm, kept_hbm,
                new_ref, image_ref, speed_ref, restarted_ref, ang_ref, ax_ref,
                buf_ref, cells_ref, field_ref, acc_ref, edge_ref, part_ref, got_ref, sum_ref, ang_buf, ax_buf, raw_ref,
                near_ref, rim_ref, rayleigh_ref, order_ref, kept_ref, load_sem, small_sem, send_sem, recv_sem):
    small = [pltpu.make_async_copy(src, dst, small_sem.at[i]) for i, (src, dst) in enumerate((
        (speed_hbm, speed_ref), (rim_hbm, rim_ref), (rayleigh_hbm, rayleigh_ref), (order_hbm, order_ref), (kept_hbm, kept_ref)))]
    for copy in small:
        copy.start()
    refs = (right_ref, left_ref)
    sector, slab = lax.axis_index("sector"), lax.axis_index("slab")
    x, y, z, core = place(sector, slab)
    other = device(x, y, z, 1 - core)
    groups = (
        (x, [device(lax.rem(x + o, 4), y, z, core) for o in (1, 2, 3)]),
        (y, [device(x, lax.rem(y + o, 4), z, core) for o in (1, 2, 3)]),
        (z, [device(x, y, lax.rem(z + o, 4), core) for o in (1, 2, 3)]),
    )
    ang_to = ((lax.rem(sector + 15, 16), slab), (lax.rem(sector + 1, 16), slab))
    ax_to = ((sector, lax.rem(slab + 7, 8)), (sector, lax.rem(slab + 1, 8)))
    exists = (slab > 0, slab < 7)

    @pl.loop(0, CA)
    def _(i):
        a = lax.rem(CA - i, CA)
        for n in range(2):
            for t in range(CT):
                for j in range(2):
                    pltpu.make_async_copy(refs[n].at[:, a, j, t, :], buf_ref.at[a, t, n, j], load_sem.at[a]).start()

    barrier = pltpu.get_barrier_semaphore()
    for peer in [other] + [p for _, peers in groups for p in peers] + list(ang_to + ax_to):
        pl.semaphore_signal(barrier, inc=1, device_id=peer, device_id_type=MESH)

    def remote(src, dst, n, peer):
        return pltpu.make_async_remote_copy(
            src_ref=src, dst_ref=dst, send_sem=send_sem.at[n], recv_sem=recv_sem.at[n],
            device_id=peer, device_id_type=MESH)

    def early_copies(side):
        a = side * (CA - 1)
        copies = [remote(speed_ref.at[a], near_ref.at[1 - side], 13 + side, ax_to[side])]
        if EARLY:
            copies.append(remote(buf_ref.at[a, 0:EARLY], raw_ref.at[1 - side, 0:EARLY], 11 + side, ax_to[side]))
        return copies

    def later_copies(side):
        a = side * (CA - 1)
        if RAW == EARLY:
            return []
        return [remote(buf_ref.at[a, EARLY:RAW], raw_ref.at[1 - side, EARLY:RAW], 19 + side, ax_to[side])]

    for copy in small:
        copy.wait()
    acc_ref[...] = jnp.zeros_like(acc_ref)
    hot = (iota((CR, CR), 0) == rim_ref[...]).astype(BF16)

    @pl.loop(0, CA)
    def _(i):
        a = lax.rem(CA - i, CA)
        pltpu.make_async_copy(buf_ref.at[a], buf_ref.at[a], load_sem.at[a]).wait()
        for side in range(2):
            @pl.when(i == side)
            def _():
                if side == 0:
                    pl.semaphore_wait(barrier, 14)
                if True:
                    @pl.when(exists[side])
                    def _():
                        for copy in early_copies(side):
                            copy.start()

        columns = []
        for t in range(CT):
            for j in range(2):
                columns.append(stacked(buf_ref[a, t, 0, j], buf_ref[a, t, 1, j]))
        block = halves(columns)
        cells_ref[a] = block
        acc_ref[...] += mm16(block[:128], block, NT)
        for side, t in ((0, 0), (1, CT - 1)):
            scaled = halves([speed_ref[a, j, t:t + 1, :] * buf_ref[a, t, 1, j] for j in range(2)])
            edge = jnp.concatenate((block[:128, t * CR:(t + 1) * CR],) + split(scaled), axis=0)
            edge_ref[side, a] = mm16(edge, hot, NT if side else NN).astype(BF16)

    part_ref[...] = combined(acc_ref[...])

    def half(h):
        return pl.ds(pl.multiple_of(h * 32, 32), 32)

    copies = [remote(part_ref.at[half(1 - core)], got_ref.at[0, 0], 0, other)]
    copies[0].start()
    copies[0].wait_recv()
    mine, theirs = part_ref[half(core), :], got_ref[0, 0]
    total = mine + theirs
    n = 1
    for stage, (me, peers) in enumerate(groups):
        got_ref[stage + 1, me] = total
        sent = []
        for peer in peers:
            copy = remote(got_ref.at[stage + 1, me], got_ref.at[stage + 1, me], n, peer)
            copy.start()
            sent.append(copy)
            n += 1
        for copy in sent:
            copy.wait_recv()
        copies += sent
        total = (got_ref[stage + 1, 0] + got_ref[stage + 1, 1]) + (got_ref[stage + 1, 2] + got_ref[stage + 1, 3])
    sum_ref[half(core), :] = total
    copy = remote(sum_ref.at[half(core)], sum_ref.at[half(core)], n, other)
    copy.start()
    copy.wait_recv()
    copies.append(copy)

    for side in range(2):
        @pl.when(exists[side])
        def _():
            for copy in later_copies(side):
                copy.start()

    rotation, restarted = small_step(sum_ref[...] * (1.0 / CELLS), rayleigh_ref[...], order_ref[...], kept_ref[...])
    restarted_ref[...] = restarted
    rotate = rotation_blocks(rotation)

    for side in range(2):
        @pl.loop(0, CA)
        def _(a):
            ang_buf[side, a] = rotated(rotate, edge_ref[side, a])
        copy = remote(ang_buf.at[side], ang_ref.at[1 - side], 15 + side, ang_to[side])
        copy.start()
        copies.append(copy)
    ang_copies = copies[-2:]

    def speed_row(ref, t):
        return halves([ref[0, pl.ds(t, 1), :], ref[1, pl.ds(t, 1), :]])

    def ax_copy(side):
        return remote(ax_buf.at[side], ax_ref.at[1 - side, RAW:], 17 + side, ax_to[side])

    if RAW < CT:
        for side in range(2):
            a = side * (CA - 1)
            for t in range(RAW, CT):
                value = rotated(rotate, cells_ref[a, :, t * CR:(t + 1) * CR])
                ax_buf[side, t - RAW, 0:KEEP] = value[:KEEP]
                ax_buf[side, t - RAW, KEEP:] = value[KEEP:] * speed_row(speed_ref.at[a], t)

            @pl.when(exists[side])
            def _():
                ax_copy(side).start()

    @pl.loop(0, CA)
    def _(a):
        for t in range(CT):
            value = rotated(rotate, cells_ref[a, :, t * CR:(t + 1) * CR])
            for j in range(2):
                part = value[:, j * 128:(j + 1) * 128]
                new_ref[a, t, j] = part
                field_ref[a, t, j, 0:KEEP] = part[:KEEP]
                field_ref[a, t, j, KEEP:] = part[KEEP:] * speed_ref[a, j, t:t + 1, :]

    @pl.loop(0, CA)
    def _(a):
        lanes = iota((64, 128), 1)
        below, above = jnp.maximum(a - 1, 0), jnp.minimum(a + 1, CA - 1)
        has_below, has_above = (a > 0).astype(F32), (a < CA - 1).astype(F32)
        for t in range(CT):
            mid = [field_ref[a, t, j] for j in range(2)]
            up = [pltpu.roll(m, 1, 1) for m in mid]
            down = [pltpu.roll(m, 127, 1) for m in mid]
            behind = [jnp.where(lanes == 0, 0.0, up[0]), jnp.where(lanes == 0, up[0], up[1])]
            ahead = [jnp.where(lanes == 127, down[1], down[0]), jnp.where(lanes == 127, 0.0, down[1])]
            for j in range(2):
                total = field_ref[below, t, j] * has_below + field_ref[above, t, j] * has_above + behind[j] + ahead[j]
                if t > 0:
                    total = total + field_ref[a, t - 1, j]
                if t < CT - 1:
                    total = total + field_ref[a, t + 1, j]
                applied = 6.0 * mid[j] - total
                image_ref[a, t, j, 0:KEEP] = applied[:KEEP] * speed_ref[a, j, t:t + 1, :] - mid[j][:KEEP]
                image_ref[a, t, j, KEEP:] = applied[KEEP:] - new_ref[a, t, j, KEEP:]

    for side in range(2):
        @pl.when(exists[side])
        def _():
            for copy in early_copies(1 - side) + later_copies(1 - side):
                copy.wait_recv()

            @pl.loop(0, RAW)
            def _(t):
                block = stacked(halves([raw_ref[side, t, 0, 0], raw_ref[side, t, 0, 1]]),
                                halves([raw_ref[side, t, 1, 0], raw_ref[side, t, 1, 1]]))
                value = rotated(rotate, block)
                ax_ref[side, t, 0:KEEP] = value[:KEEP]
                ax_ref[side, t, KEEP:] = value[KEEP:] * speed_row(near_ref.at[side], t)

    for side in range(2):
        ang_copies[1 - side].wait_recv()

        @pl.when(exists[side])
        def _():
            if RAW < CT:
                ax_copy(1 - side).wait_recv()
                ax_copy(side).wait_send()
            for copy in early_copies(side) + later_copies(side):
                copy.wait_send()
    for copy in copies:
        copy.wait_send()


def core_step(right, left, speed, rim, rayleigh, order, kept):
    vmem = pl.BlockSpec(memory_space=pltpu.VMEM)
    main = pl.BlockSpec(memory_space=pltpu.HBM)
    sent = max(CT - RAW, 1)
    inputs = [pltpu.with_memory_space_constraint(v, pltpu.HBM) for v in (right, left, speed, rim, rayleigh, order, kept)]
    return pl.pallas_call(
        core_kernel,
        in_specs=[main] * 7,
        out_specs=[vmem] * 6,
        out_shape=[
            pltpu.VMEM((CA, CT, 2, 64, 128), F32),
            pltpu.VMEM((CA, CT, 2, 64, 128), F32),
            pltpu.VMEM((CA, 2, CT, 128), F32),
            pltpu.VMEM((KEEP, KEEP), F32),
            pltpu.VMEM((2, CA, 64, CR), F32),
            pltpu.VMEM((2, CT, 64, CR), F32),
        ],
        scratch_shapes=[
            pltpu.VMEM((CA, CT, 2, 2, 64, 128), F32),
            pltpu.VMEM((CA, 256, CT * CR), BF16),
            pltpu.VMEM((CA, CT, 2, 64, 128), F32),
            pltpu.VMEM((128, 256), F32),
            pltpu.VMEM((2, CA, 256, CR), BF16),
            pltpu.VMEM((64, 128), F32),
            pltpu.VMEM((4, 4, 32, 128), F32),
            pltpu.VMEM((64, 128), F32),
            pltpu.VMEM((2, CA, 64, CR), F32),
            pltpu.VMEM((2, sent, 64, CR), F32),
            pltpu.VMEM((2, RAW, 2, 2, 64, 128), F32),
            pltpu.VMEM((2, 2, CT, 128), F32),
            pltpu.VMEM((1, CR), jnp.int32),
            pltpu.VMEM((K, K), F32),
            pltpu.VMEM((1, K), jnp.int32),
            pltpu.VMEM((1, KEEP), jnp.int32),
            pltpu.SemaphoreType.DMA((CA,)),
            pltpu.SemaphoreType.DMA((5,)),
            pltpu.SemaphoreType.DMA((21,)),
            pltpu.SemaphoreType.DMA((21,)),
        ],
        compiler_params=pltpu.CompilerParams(collective_id=0, has_side_effects=True, vmem_limit_bytes=44 << 20),
        name="core",
    )(*inputs)


def finish_kernel(new_ref, image_ref, speed_ref, restarted_in, ang_ref, ax_ref, new_right_ref, new_left_ref,
                  right_image_ref, left_image_ref, restarted_ref, fix_ref, sem):
    slab = lax.axis_index("slab")
    outs = (new_right_ref, new_left_ref, right_image_ref, left_image_ref)

    def send(n, src, a, t):
        for j in range(2):
            low = (n % 2) * KEEP
            pltpu.make_async_copy(src.at[t, j, low:low + KEEP], outs[n].at[:, a, j, t, :], sem.at[n]).start()

    @pl.loop(0, CA)
    def _(a):
        for t in range(CT):
            send(0, new_ref.at[a], a, t)
            send(1, new_ref.at[a], a, t)

    @pl.loop(1, CA - 1)
    def _(a):
        for t in range(1, CT - 1):
            send(2, image_ref.at[a], a, t)
            send(3, image_ref.at[a], a, t)

    @pl.loop(0, CA)
    def _(a):
        def fix(t):
            for j in range(2):
                lanes = slice(j * 128, (j + 1) * 128)
                halo = jnp.zeros((64, 128), F32)
                if t == 0:
                    halo = halo + ang_ref[0, a, :, lanes]
                if t == CT - 1:
                    halo = halo + ang_ref[1, a, :, lanes]
                halo = halo + jnp.where(jnp.logical_and(a == 0, slab > 0), ax_ref[0, t, :, lanes], 0.0)
                halo = halo + jnp.where(jnp.logical_and(a == CA - 1, slab < 7), ax_ref[1, t, :, lanes], 0.0)
                value = image_ref[a, t, j]
                fix_ref[a, t, j, 0:KEEP] = value[:KEEP] - halo[:KEEP] * speed_ref[a, j, t:t + 1, :]
                fix_ref[a, t, j, KEEP:] = value[KEEP:] - halo[KEEP:]
            send(2, fix_ref.at[a], a, t)
            send(3, fix_ref.at[a], a, t)

        for t in (0, CT - 1):
            fix(t)

        @pl.when(jnp.logical_or(a == 0, a == CA - 1))
        def _():
            for t in range(1, CT - 1):
                fix(t)

    restarted_ref[...] = restarted_in[...]
    for n in range(4):
        pltpu.make_async_copy(outs[n], outs[n], sem.at[n]).wait()


def finish(*arrays):
    vmem = pl.BlockSpec(memory_space=pltpu.VMEM)
    main = pl.BlockSpec(memory_space=pltpu.HBM)
    kept = jax.ShapeDtypeStruct((KEEP, CA, 2, CT, 128), F32)
    return pl.pallas_call(
        finish_kernel,
        in_specs=[vmem] * 6,
        out_specs=[main] * 4 + [vmem],
        out_shape=[kept] * 4 + [jax.ShapeDtypeStruct((KEEP, KEEP), F32)],
        scratch_shapes=[pltpu.VMEM((CA, CT, 2, 64, 128), F32), pltpu.SemaphoreType.DMA((4,))],
        compiler_params=pltpu.CompilerParams(vmem_limit_bytes=10 << 20),
        name="finish",
    )(*[pltpu.with_memory_space_constraint(v, pltpu.VMEM) for v in arrays])


def tiles(array):
    return array.reshape(array.shape[0], CT, CA, 2, 128).transpose(0, 2, 3, 1, 4)


def local(right_basis, left_basis, speed_squared, rayleigh, schur_order, kept_index, rim_map):
    right, left, speed = tiles(right_basis), tiles(left_basis), tiles(speed_squared[None])[0]
    *outs, restarted = finish(*core_step(
        right, left, speed, rim_map.reshape(1, CR), rayleigh, schur_order.reshape(1, K), kept_index.reshape(1, KEEP)))
    shape = (KEEP, CT, CA, CR)
    return tuple(o.transpose(0, 3, 1, 2, 4).reshape(shape) for o in outs) + (restarted,)


def solution(mesh):
    fields = P(None, "sector", "slab", None)
    return jax.shard_map(
        local,
        mesh=mesh,
        in_specs=(fields, fields, P("sector", "slab", None), P(), P(), P(), P()),
        out_specs=(fields, fields, fields, fields, P()),
        check_vma=False,
    )
```

time: 514 us -> 74.8 us (0.15); the launches traced: 506 us -> 74.4 us
  local copies, waits for them, and re-layouts: 133 us -> 0 us
  blocking collectives: 132 us -> 0 us
  matrix products: 119 us -> 0 us
  Pallas kernels: 0 us -> 73.7 us
  other arithmetic: 66 us -> 0 us
  loops' own time: 45.8 us -> 0 us
  starting transfers between devices: 9.64 us -> 0 us
    psum x2 -> x0, blocking collectives: 132 us -> none  [the longest x1 69 us: local(): lax.psum(exact_dot(right_rows, right_rows.T), ('sector', 'slab'))]
    dot_general x271 -> x0, matrix products: 118 us -> none  [exact_dot(): jnp.dot(left_operator, right_operator, precision=lax.Precision.HIGHEST)]
    pallas_call x0 -> x2, Pallas kernels: none -> 73.7 us  [the longest x1 68.7 us: core_step(): pl.pallas_call(core_kernel, in_specs=[main] * 7, out_specs=[vmem] * 6, ou...]
    another operation x1 -> x0, loops' own time: 45.8 us -> none  [orthonormal(): lax.fori_loop(0, matrix.shape[1], column_step, jnp.zeros_like(matrix))]
    unnamed x27 -> x0, local copies, waits for them, and re-layouts: 39.8 us -> none
    reshape x7 -> x0, local copies, waits for them, and re-layouts: 34.4 us -> none  [the longest x1 7.01 us: local(): stacked.reshape((2 * kept_count,) + grid_shape)]
    slice x8 -> x0, local copies, waits for them, and re-layouts: 33.7 us -> none  [the longest x1 12.2 us: laplace(): vector_columns[:, :-1]]
    sub x3 -> x0, other arithmetic: 31.8 us -> none  [the longest x1 23 us: laplace(): return final_result - padded[..., 2:] - padded[..., :-2]]
  transfers between devices with their start and end apart: 4 -> 0, of which waited for: 0 -> 0; matrix products, arithmetic and copies ran while one was open for 13% -> 0% of each run, Pallas kernels for 0% -> 0%
where the time goes in v2:
time: 74.8 us; the launch traced here: 74.4 us
  Pallas kernels  73.7 us (99%)
    pallas_call x1, Pallas kernels, core_step(): pl.pallas_call(core_kernel, in_specs=[main] * 7, out_specs=[vmem] * 6, ou...  68.7 us
    pallas_call x1, Pallas kernels, finish(): pl.pallas_call(finish_kernel, in_specs=[vmem] * 6, out_specs=[main] * 4 +...  5.03 us

profile of v2, /device:TPU:1, one launch (start us, length us, event | category | flops | bytes accessed | tf_op | source)
XLA Modules:
  0.0 74.4 jit_solution(14728046396726304120)
XLA Ops:
  0.6 68.7 %core.1 = (f32[12,8,2,64,128]{4,3,2,1,0:T(8,128)S(1)}, f32[12,8,2,64,128]{4,3,2,1,0:T(8,128)S(1)}, f32[12,2,8,128]{3,2,1,0:T(8,128)S(1)}, f32[32,32]{1,0:T(8,128...) custom-call(f32[64,12,2,8,128]{4,3,2,1,0:T(8,128)} %bitcast.26, f32[64,12,2,8,128]{4,3,2,1,0:T(8,128)} %bitcast.27, ...), custom_call_target="tpu_custom_call" | custom-call | tf_op jit(solution)/shard_map/core/pallas_call | solution.py:368
  69.3 5.0 %finish.1 = (f32[32,12,2,8,128]{4,3,2,1,0:T(8,128)}, f32[32,12,2,8,128]{4,3,2,1,0:T(8,128)}, f32[32,12,2,8,128]{4,3,2,1,0:T(8,128)}, f32[32,12,2,8,128]{4,3,2,1,0:T(8,128)}, f32[32,32]{1,0:T(8,128)}) custom-call(f32[12,8,2,64,128]{4,3,2,1,0:T(8,128)S(1)} %get-tuple-element.16.new_ref, f32[12,8,2,64,128]{4,3,2,1,0:T(8,128)S(1)} %get-tuple-element.17.image_ref, ...), custom_call_target="tpu_custom_call" | custom-call | tf_op jit(solution)/shard_map/finish/pallas_call | solution.py:464

commit v3 on v2

--- a/solution.py
+++ b/solution.py
@@ -13,8 +13,8 @@
 BF16 = jnp.bfloat16
 K, KEEP, CT, CA, CR = 64, 32, 8, 12, 256
 CELLS = 3145728
-EARLY = 2
-RAW = 4
+SENT = (6, 6, 6, 6, 6, 6, 8)
+RAW = SENT[-1] // 2
 
 
 def mm(a, b, dims=NN):
@@ -126,11 +126,12 @@
     tail = jnp.concatenate([lower_inv, mm(lower_t, cross_inv)], axis=1)
     basis_t = eliminate([a3])[0][:, 64:]
     weight = jnp.where(r64 > c64, 1.0, jnp.where(r64 == c64, 0.5, 0.0))
-    for _ in range(2):
-        basis_t = basis_t - mm((mm(basis_t, basis_t, NT) - eye) * weight, basis_t)
-    kept_t = mm(select_kept, basis_t)
+    basis_t = basis_t - mm((mm(basis_t, basis_t, NT) - eye) * weight, basis_t)
+    change = (mm(basis_t, basis_t, NT) - eye) * weight
+    chosen = select_kept - mm(select_kept, change)
+    kept_t = mm(chosen, basis_t)
     restarted = mm(mm(kept_t, permuted_t, NT), kept_t, NT)
-    return mm(kept_t, tail), restarted
+    return mm(chosen, mm(basis_t, tail)), restarted
 
 
 def rotation_blocks(rotation):
@@ -179,7 +180,7 @@
         for n in range(2):
             for t in range(CT):
                 for j in range(2):
-                    pltpu.make_async_copy(refs[n].at[:, a, j, t, :], buf_ref.at[a, t, n, j], load_sem.at[a]).start()
+                    pltpu.make_async_copy(refs[n].at[:, a, j, t, :], buf_ref.at[a, 2 * t + n, j], load_sem.at[a]).start()
 
     barrier = pltpu.get_barrier_semaphore()
     for peer in [other] + [p for _, peers in groups for p in peers] + list(ang_to + ax_to):
@@ -190,18 +191,26 @@
             src_ref=src, dst_ref=dst, send_sem=send_sem.at[n], recv_sem=recv_sem.at[n],
             device_id=peer, device_id_type=MESH)
 
-    def early_copies(side):
+    def near_copy(side):
+        return remote(speed_ref.at[side * (CA - 1)], near_ref.at[1 - side], 11 + side, ax_to[side])
+
+    def raw_copies(side, stage=None):
         a = side * (CA - 1)
-        copies = [remote(speed_ref.at[a], near_ref.at[1 - side], 13 + side, ax_to[side])]
-        if EARLY:
-            copies.append(remote(buf_ref.at[a, 0:EARLY], raw_ref.at[1 - side, 0:EARLY], 11 + side, ax_to[side]))
+        copies = []
+        for i in range(len(SENT)):
+            units = slice(SENT[i - 1] if i else 0, SENT[i])
+            if units.start < units.stop and stage in (None, i):
+                copies.append(remote(buf_ref.at[a, units], raw_ref.at[1 - side, units], 19 + 2 * i + side, ax_to[side]))
         return copies
 
-    def later_copies(side):
-        a = side * (CA - 1)
-        if RAW == EARLY:
-            return []
-        return [remote(buf_ref.at[a, EARLY:RAW], raw_ref.at[1 - side, EARLY:RAW], 19 + side, ax_to[side])]
+    def send_raw(stage):
+        if stage and SENT[stage] == SENT[stage - 1]:
+            return
+        for side in range(2):
+            @pl.when(exists[side])
+            def _():
+                for copy in raw_copies(side, stage):
+                    copy.start()
 
     for copy in small:
         copy.wait()
@@ -220,28 +229,35 @@
                 if True:
                     @pl.when(exists[side])
                     def _():
-                        for copy in early_copies(side):
+                        for copy in [near_copy(side)] + raw_copies(side, 0):
                             copy.start()
 
         columns = []
         for t in range(CT):
             for j in range(2):
-                columns.append(stacked(buf_ref[a, t, 0, j], buf_ref[a, t, 1, j]))
+                columns.append(stacked(buf_ref[a, 2 * t, j], buf_ref[a, 2 * t + 1, j]))
         block = halves(columns)
         cells_ref[a] = block
         acc_ref[...] += mm16(block[:128], block, NT)
-        for side, t in ((0, 0), (1, CT - 1)):
-            scaled = halves([speed_ref[a, j, t:t + 1, :] * buf_ref[a, t, 1, j] for j in range(2)])
-            edge = jnp.concatenate((block[:128, t * CR:(t + 1) * CR],) + split(scaled), axis=0)
+
+    part_ref[...] = combined(acc_ref[...])
+
+    def edges(side):
+        t = side * (CT - 1)
+
+        @pl.loop(0, CA)
+        def _(a):
+            scaled = halves([speed_ref[a, j, t:t + 1, :] * buf_ref[a, 2 * t + 1, j] for j in range(2)])
+            edge = jnp.concatenate((cells_ref[a, 0:128, t * CR:(t + 1) * CR],) + split(scaled), axis=0)
             edge_ref[side, a] = mm16(edge, hot, NT if side else NN).astype(BF16)
-
-    part_ref[...] = combined(acc_ref[...])
 
     def half(h):
         return pl.ds(pl.multiple_of(h * 32, 32), 32)
 
     copies = [remote(part_ref.at[half(1 - core)], got_ref.at[0, 0], 0, other)]
     copies[0].start()
+    send_raw(1)
+    edges(0)
     copies[0].wait_recv()
     mine, theirs = part_ref[half(core), :], got_ref[0, 0]
     total = mine + theirs
@@ -254,6 +270,9 @@
             copy.start()
             sent.append(copy)
             n += 1
+        send_raw(stage + 2)
+        if stage == 0:
+            edges(1)
         for copy in sent:
             copy.wait_recv()
         copies += sent
@@ -261,18 +280,32 @@
     sum_ref[half(core), :] = total
     copy = remote(sum_ref.at[half(core)], sum_ref.at[half(core)], n, other)
     copy.start()
+    send_raw(5)
     copy.wait_recv()
     copies.append(copy)
 
-    for side in range(2):
-        @pl.when(exists[side])
-        def _():
-            for copy in later_copies(side):
-                copy.start()
-
+    send_raw(6)
     rotation, restarted = small_step(sum_ref[...] * (1.0 / CELLS), rayleigh_ref[...], order_ref[...], kept_ref[...])
     restarted_ref[...] = restarted
     rotate = rotation_blocks(rotation)
+
+    def speed_row(ref, t):
+        return halves([ref[0, pl.ds(t, 1), :], ref[1, pl.ds(t, 1), :]])
+
+    def ax_copy(side):
+        return remote(ax_buf.at[side], ax_ref.at[1 - side, RAW:], 17 + side, ax_to[side])
+
+    if RAW < CT:
+        for side in range(2):
+            a = side * (CA - 1)
+            for t in range(RAW, CT):
+                value = rotated(rotate, cells_ref[a, :, t * CR:(t + 1) * CR])
+                ax_buf[side, t - RAW, 0:KEEP] = value[:KEEP]
+                ax_buf[side, t - RAW, KEEP:] = value[KEEP:] * speed_row(speed_ref.at[a], t)
+
+            @pl.when(exists[side])
+            def _():
+                ax_copy(side).start()
 
     for side in range(2):
         @pl.loop(0, CA)
@@ -282,24 +315,6 @@
         copy.start()
         copies.append(copy)
     ang_copies = copies[-2:]
-
-    def speed_row(ref, t):
-        return halves([ref[0, pl.ds(t, 1), :], ref[1, pl.ds(t, 1), :]])
-
-    def ax_copy(side):
-        return remote(ax_buf.at[side], ax_ref.at[1 - side, RAW:], 17 + side, ax_to[side])
-
-    if RAW < CT:
-        for side in range(2):
-            a = side * (CA - 1)
-            for t in range(RAW, CT):
-                value = rotated(rotate, cells_ref[a, :, t * CR:(t + 1) * CR])
-                ax_buf[side, t - RAW, 0:KEEP] = value[:KEEP]
-                ax_buf[side, t - RAW, KEEP:] = value[KEEP:] * speed_row(speed_ref.at[a], t)
-
-            @pl.when(exists[side])
-            def _():
-                ax_copy(side).start()
 
     @pl.loop(0, CA)
     def _(a):
@@ -335,13 +350,13 @@
     for side in range(2):
         @pl.when(exists[side])
         def _():
-            for copy in early_copies(1 - side) + later_copies(1 - side):
+            for copy in [near_copy(1 - side)] + raw_copies(1 - side):
                 copy.wait_recv()
 
             @pl.loop(0, RAW)
             def _(t):
-                block = stacked(halves([raw_ref[side, t, 0, 0], raw_ref[side, t, 0, 1]]),
-                                halves([raw_ref[side, t, 1, 0], raw_ref[side, t, 1, 1]]))
+                block = stacked(halves([raw_ref[side, 2 * t, 0], raw_ref[side, 2 * t, 1]]),
+                                halves([raw_ref[side, 2 * t + 1, 0], raw_ref[side, 2 * t + 1, 1]]))
                 value = rotated(rotate, block)
                 ax_ref[side, t, 0:KEEP] = value[:KEEP]
                 ax_ref[side, t, KEEP:] = value[KEEP:] * speed_row(near_ref.at[side], t)
@@ -354,7 +369,7 @@
             if RAW < CT:
                 ax_copy(1 - side).wait_recv()
                 ax_copy(side).wait_send()
-            for copy in early_copies(side) + later_copies(side):
+            for copy in [near_copy(side)] + raw_copies(side):
                 copy.wait_send()
     for copy in copies:
         copy.wait_send()
@@ -378,7 +393,7 @@
             pltpu.VMEM((2, CT, 64, CR), F32),
         ],
         scratch_shapes=[
-            pltpu.VMEM((CA, CT, 2, 2, 64, 128), F32),
+            pltpu.VMEM((CA, 2 * CT, 2, 64, 128), F32),
             pltpu.VMEM((CA, 256, CT * CR), BF16),
             pltpu.VMEM((CA, CT, 2, 64, 128), F32),
             pltpu.VMEM((128, 256), F32),
@@ -388,7 +403,7 @@
             pltpu.VMEM((64, 128), F32),
             pltpu.VMEM((2, CA, 64, CR), F32),
             pltpu.VMEM((2, sent, 64, CR), F32),
-            pltpu.VMEM((2, RAW, 2, 2, 64, 128), F32),
+            pltpu.VMEM((2, 2 * RAW, 2, 64, 128), F32),
             pltpu.VMEM((2, 2, CT, 128), F32),
             pltpu.VMEM((1, CR), jnp.int32),
             pltpu.VMEM((K, K), F32),
@@ -396,8 +411,8 @@
             pltpu.VMEM((1, KEEP), jnp.int32),
             pltpu.SemaphoreType.DMA((CA,)),
             pltpu.SemaphoreType.DMA((5,)),
-            pltpu.SemaphoreType.DMA((21,)),
-            pltpu.SemaphoreType.DMA((21,)),
+            pltpu.SemaphoreType.DMA((33,)),
+            pltpu.SemaphoreType.DMA((33,)),
         ],
         compiler_params=pltpu.CompilerParams(collective_id=0, has_side_effects=True, vmem_limit_bytes=44 << 20),
         name="core",

time: 74.8 us -> 72.3 us (0.967)
  Pallas kernels: 73.7 us -> 71.6 us
    pallas_call x1, Pallas kernels: 68.7 us -> 66.6 us  [core_step(): pl.pallas_call(core_kernel, in_specs=[main] * 7, out_specs=[vmem] * 6, ou...]
where the time goes in v3:
time: 72.3 us; the launch traced here: 72.2 us
  Pallas kernels  71.6 us (99%)
    pallas_call x1, Pallas kernels, core_step(): pl.pallas_call(core_kernel, in_specs=[main] * 7, out_specs=[vmem] * 6, ou...  66.6 us
    pallas_call x1, Pallas kernels, finish(): pl.pallas_call(finish_kernel, in_specs=[vmem] * 6, out_specs=[main] * 4 +...  5.03 us

profile of v3, /device:TPU:1, one launch (start us, length us, event | category | flops | bytes accessed | tf_op | source)
XLA Modules:
  0.0 72.2 jit_solution(14115165444112418080)
XLA Ops:
  0.6 66.6 %core.1 = (f32[12,8,2,64,128]{4,3,2,1,0:T(8,128)S(1)}, f32[12,8,2,64,128]{4,3,2,1,0:T(8,128)S(1)}, f32[12,2,8,128]{3,2,1,0:T(8,128)S(1)}, f32[32,32]{1,0:T(8,128...) custom-call(f32[64,12,2,8,128]{4,3,2,1,0:T(8,128)} %bitcast.26, f32[64,12,2,8,128]{4,3,2,1,0:T(8,128)} %bitcast.27, ...), custom_call_target="tpu_custom_call" | custom-call | tf_op jit(solution)/shard_map/core/pallas_call | solution.py:383
  67.2 5.0 %finish.1 = (f32[32,12,2,8,128]{4,3,2,1,0:T(8,128)}, f32[32,12,2,8,128]{4,3,2,1,0:T(8,128)}, f32[32,12,2,8,128]{4,3,2,1,0:T(8,128)}, f32[32,12,2,8,128]{4,3,2,1,0:T(8,128)}, f32[32,32]{1,0:T(8,128)}) custom-call(f32[12,8,2,64,128]{4,3,2,1,0:T(8,128)S(1)} %get-tuple-element.16.new_ref, f32[12,8,2,64,128]{4,3,2,1,0:T(8,128)S(1)} %get-tuple-element.17.image_ref, ...), custom_call_target="tpu_custom_call" | custom-call | tf_op jit(solution)/shard_map/finish/pallas_call | solution.py:479

commit v4 on v3

--- a/solution.py
+++ b/solution.py
@@ -13,7 +13,7 @@
 BF16 = jnp.bfloat16
 K, KEEP, CT, CA, CR = 64, 32, 8, 12, 256
 CELLS = 3145728
-SENT = (6, 6, 6, 6, 6, 6, 8)
+SENT = (6, 8)
 RAW = SENT[-1] // 2
 
 
@@ -155,7 +155,7 @@
 
 def core_kernel(right_ref, left_ref, speed_hbm, rim_hbm, rayleigh_hbm, order_hbm, kept_hbm,
                 new_ref, image_ref, speed_ref, restarted_ref, ang_ref, ax_ref,
-                buf_ref, cells_ref, field_ref, acc_ref, edge_ref, part_ref, got_ref, sum_ref, ang_buf, ax_buf, raw_ref,
+                buf_ref, cells_ref, field_ref, acc_ref, edge_ref, part_ref, row_ref, line_ref, column_ref, sum_ref, ang_buf, ax_buf, raw_ref,
                 near_ref, rim_ref, rayleigh_ref, order_ref, kept_ref, load_sem, small_sem, send_sem, recv_sem):
     small = [pltpu.make_async_copy(src, dst, small_sem.at[i]) for i, (src, dst) in enumerate((
         (speed_hbm, speed_ref), (rim_hbm, rim_ref), (rayleigh_hbm, rayleigh_ref), (order_hbm, order_ref), (kept_hbm, kept_ref)))]
@@ -164,12 +164,19 @@
     refs = (right_ref, left_ref)
     sector, slab = lax.axis_index("sector"), lax.axis_index("slab")
     x, y, z, core = place(sector, slab)
-    other = device(x, y, z, 1 - core)
-    groups = (
-        (x, [device(lax.rem(x + o, 4), y, z, core) for o in (1, 2, 3)]),
-        (y, [device(x, lax.rem(y + o, 4), z, core) for o in (1, 2, 3)]),
-        (z, [device(x, y, lax.rem(z + o, 4), core) for o in (1, 2, 3)]),
-    )
+    lane, column = 2 * x + core, 2 * z + core
+
+    def in_row(o):
+        other = lax.rem(lane + o, 8)
+        return lax.rem(other, 2), device(other // 2, y, z, lax.rem(other, 2))
+
+    def in_line(o):
+        return device(x, lax.rem(y + o, 4), z, core)
+
+    def in_column(o):
+        other = lax.rem(column + o, 8)
+        return device(x, y, other // 2, lax.rem(other, 2))
+
     ang_to = ((lax.rem(sector + 15, 16), slab), (lax.rem(sector + 1, 16), slab))
     ax_to = ((sector, lax.rem(slab + 7, 8)), (sector, lax.rem(slab + 1, 8)))
     exists = (slab > 0, slab < 7)
@@ -183,7 +190,8 @@
                     pltpu.make_async_copy(refs[n].at[:, a, j, t, :], buf_ref.at[a, 2 * t + n, j], load_sem.at[a]).start()
 
     barrier = pltpu.get_barrier_semaphore()
-    for peer in [other] + [p for _, peers in groups for p in peers] + list(ang_to + ax_to):
+    for peer in ([in_row(o)[1] for o in range(1, 8)] + [in_line(o) for o in range(1, 4)]
+                 + [in_column(o) for o in range(1, 8)] + list(ang_to + ax_to)):
         pl.semaphore_signal(barrier, inc=1, device_id=peer, device_id_type=MESH)
 
     def remote(src, dst, n, peer):
@@ -225,7 +233,7 @@
             @pl.when(i == side)
             def _():
                 if side == 0:
-                    pl.semaphore_wait(barrier, 14)
+                    pl.semaphore_wait(barrier, 21)
                 if True:
                     @pl.when(exists[side])
                     def _():
@@ -254,37 +262,41 @@
     def half(h):
         return pl.ds(pl.multiple_of(h * 32, 32), 32)
 
-    copies = [remote(part_ref.at[half(1 - core)], got_ref.at[0, 0], 0, other)]
-    copies[0].start()
+    def summed(ref, *lead):
+        parts = [ref[lead + (i,)] for i in range(ref.shape[len(lead)])]
+        while len(parts) > 1:
+            parts = [parts[i] + parts[i + 1] for i in range(0, len(parts), 2)]
+        return parts[0]
+
+    copies = []
+
+    def spread(n, src, dst, peer):
+        copy = remote(src, dst, n, peer)
+        copy.start()
+        copies.append(copy)
+
+    for o in range(1, 8):
+        side, peer = in_row(o)
+        spread(o - 1, part_ref.at[half(side)], row_ref.at[lane], peer)
+    row_ref[lane] = part_ref[half(core), :]
+    edges(0)
+    for copy in copies[:7]:
+        copy.wait_recv()
+    line_ref[y] = summed(row_ref)
+    for o in range(1, 4):
+        spread(6 + o, line_ref.at[y], line_ref.at[y], in_line(o))
+    edges(1)
+    for copy in copies[7:10]:
+        copy.wait_recv()
+    column_ref[core, z] = summed(line_ref)
+    for o in range(1, 8):
+        spread(32 + o, column_ref.at[core, z], column_ref.at[core, z], in_column(o))
+    for copy in copies[10:]:
+        copy.wait_recv()
+    for side in range(2):
+        sum_ref[side * 32:(side + 1) * 32, :] = summed(column_ref, side)
+
     send_raw(1)
-    edges(0)
-    copies[0].wait_recv()
-    mine, theirs = part_ref[half(core), :], got_ref[0, 0]
-    total = mine + theirs
-    n = 1
-    for stage, (me, peers) in enumerate(groups):
-        got_ref[stage + 1, me] = total
-        sent = []
-        for peer in peers:
-            copy = remote(got_ref.at[stage + 1, me], got_ref.at[stage + 1, me], n, peer)
-            copy.start()
-            sent.append(copy)
-            n += 1
-        send_raw(stage + 2)
-        if stage == 0:
-            edges(1)
-        for copy in sent:
-            copy.wait_recv()
-        copies += sent
-        total = (got_ref[stage + 1, 0] + got_ref[stage + 1, 1]) + (got_ref[stage + 1, 2] + got_ref[stage + 1, 3])
-    sum_ref[half(core), :] = total
-    copy = remote(sum_ref.at[half(core)], sum_ref.at[half(core)], n, other)
-    copy.start()
-    send_raw(5)
-    copy.wait_recv()
-    copies.append(copy)
-
-    send_raw(6)
     rotation, restarted = small_step(sum_ref[...] * (1.0 / CELLS), rayleigh_ref[...], order_ref[...], kept_ref[...])
     restarted_ref[...] = restarted
     rotate = rotation_blocks(rotation)
@@ -399,7 +411,9 @@
             pltpu.VMEM((128, 256), F32),
             pltpu.VMEM((2, CA, 256, CR), BF16),
             pltpu.VMEM((64, 128), F32),
-            pltpu.VMEM((4, 4, 32, 128), F32),
+            pltpu.VMEM((8, 32, 128), F32),
+            pltpu.VMEM((4, 32, 128), F32),
+            pltpu.VMEM((2, 4, 32, 128), F32),
             pltpu.VMEM((64, 128), F32),
             pltpu.VMEM((2, CA, 64, CR), F32),
             pltpu.VMEM((2, sent, 64, CR), F32),
@@ -411,8 +425,8 @@
             pltpu.VMEM((1, KEEP), jnp.int32),
             pltpu.SemaphoreType.DMA((CA,)),
             pltpu.SemaphoreType.DMA((5,)),
-            pltpu.SemaphoreType.DMA((33,)),
-            pltpu.SemaphoreType.DMA((33,)),
+            pltpu.SemaphoreType.DMA((41,)),
+            pltpu.SemaphoreType.DMA((41,)),
         ],
         compiler_params=pltpu.CompilerParams(collective_id=0, has_side_effects=True, vmem_limit_bytes=44 << 20),
         name="core",

time: 72.3 us -> 71.4 us (0.988)
  Pallas kernels: 71.6 us -> 70.1 us
    pallas_call x1, Pallas kernels: 66.6 us -> 65.1 us  [core_step(): pl.pallas_call(core_kernel, in_specs=[main] * 7, out_specs=[vmem] * 6, ou...]
where the time goes in v4:
time: 71.4 us; the launch traced here: 70.7 us
  Pallas kernels  70.1 us (98%)
    pallas_call x1, Pallas kernels, core_step(): pl.pallas_call(core_kernel, in_specs=[main] * 7, out_specs=[vmem] * 6, ou...  65.1 us
    pallas_call x1, Pallas kernels, finish(): pl.pallas_call(finish_kernel, in_specs=[vmem] * 6, out_specs=[main] * 4 +...  5.03 us

profile of v4, /device:TPU:1, one launch (start us, length us, event | category | flops | bytes accessed | tf_op | source)
XLA Modules:
  0.0 70.7 jit_solution(16429484832954629182)
XLA Ops:
  0.6 65.1 %core.1 = (f32[12,8,2,64,128]{4,3,2,1,0:T(8,128)S(1)}, f32[12,8,2,64,128]{4,3,2,1,0:T(8,128)S(1)}, f32[12,2,8,128]{3,2,1,0:T(8,128)S(1)}, f32[32,32]{1,0:T(8,128...) custom-call(f32[64,12,2,8,128]{4,3,2,1,0:T(8,128)} %bitcast.26, f32[64,12,2,8,128]{4,3,2,1,0:T(8,128)} %bitcast.27, ...), custom_call_target="tpu_custom_call" | custom-call | tf_op jit(solution)/shard_map/core/pallas_call | solution.py:395
  65.7 5.0 %finish.1 = (f32[32,12,2,8,128]{4,3,2,1,0:T(8,128)}, f32[32,12,2,8,128]{4,3,2,1,0:T(8,128)}, f32[32,12,2,8,128]{4,3,2,1,0:T(8,128)}, f32[32,12,2,8,128]{4,3,2,1,0:T(8,128)}, f32[32,32]{1,0:T(8,128)}) custom-call(f32[12,8,2,64,128]{4,3,2,1,0:T(8,128)S(1)} %get-tuple-element.16.new_ref, f32[12,8,2,64,128]{4,3,2,1,0:T(8,128)S(1)} %get-tuple-element.17.image_ref, ...), custom_call_target="tpu_custom_call" | custom-call | tf_op jit(solution)/shard_map/finish/pallas_call | solution.py:493

commit v5 on v4

--- a/solution.py
+++ b/solution.py
@@ -15,6 +15,7 @@
 CELLS = 3145728
 SENT = (6, 8)
 RAW = SENT[-1] // 2
+AHEAD = 4
 
 
 def mm(a, b, dims=NN):
@@ -181,18 +182,21 @@
     ax_to = ((sector, lax.rem(slab + 7, 8)), (sector, lax.rem(slab + 1, 8)))
     exists = (slab > 0, slab < 7)
 
-    @pl.loop(0, CA)
-    def _(i):
+    barrier = pltpu.get_barrier_semaphore()
+    for peer in ([in_row(o)[1] for o in range(1, 8)] + [in_line(o) for o in range(1, 4)]
+                 + [in_column(o) for o in range(1, 8)] + list(ang_to + ax_to)):
+        pl.semaphore_signal(barrier, inc=1, device_id=peer, device_id_type=MESH)
+
+    def load(i):
         a = lax.rem(CA - i, CA)
         for n in range(2):
             for t in range(CT):
                 for j in range(2):
                     pltpu.make_async_copy(refs[n].at[:, a, j, t, :], buf_ref.at[a, 2 * t + n, j], load_sem.at[a]).start()
 
-    barrier = pltpu.get_barrier_semaphore()
-    for peer in ([in_row(o)[1] for o in range(1, 8)] + [in_line(o) for o in range(1, 4)]
-                 + [in_column(o) for o in range(1, 8)] + list(ang_to + ax_to)):
-        pl.semaphore_signal(barrier, inc=1, device_id=peer, device_id_type=MESH)
+    @pl.loop(0, AHEAD)
+    def _(i):
+        load(i)
 
     def remote(src, dst, n, peer):
         return pltpu.make_async_remote_copy(
@@ -228,6 +232,11 @@
     @pl.loop(0, CA)
     def _(i):
         a = lax.rem(CA - i, CA)
+
+        @pl.when(i + AHEAD < CA)
+        def _():
+            load(i + AHEAD)
+
         pltpu.make_async_copy(buf_ref.at[a], buf_ref.at[a], load_sem.at[a]).wait()
         for side in range(2):
             @pl.when(i == side)

time: 71.4 us -> 70.4 us (0.986)
  Pallas kernels: 70.1 us -> 69.1 us
    pallas_call x1, Pallas kernels: 65.1 us -> 64 us  [core_step(): pl.pallas_call(core_kernel, in_specs=[main] * 7, out_specs=[vmem] * 6, ou...]
where the time goes in v5:
time: 70.4 us; the launch traced here: 69.7 us
  Pallas kernels  69.1 us (98%)
    pallas_call x1, Pallas kernels, core_step(): pl.pallas_call(core_kernel, in_specs=[main] * 7, out_specs=[vmem] * 6, ou...  64 us
    pallas_call x1, Pallas kernels, finish(): pl.pallas_call(finish_kernel, in_specs=[vmem] * 6, out_specs=[main] * 4 +...  5.03 us

profile of v5, /device:TPU:1, one launch (start us, length us, event | category | flops | bytes accessed | tf_op | source)
XLA Modules:
  0.0 69.7 jit_solution(17845962367232844974)
XLA Ops:
  0.6 64.0 %core.1 = (f32[12,8,2,64,128]{4,3,2,1,0:T(8,128)S(1)}, f32[12,8,2,64,128]{4,3,2,1,0:T(8,128)S(1)}, f32[12,2,8,128]{3,2,1,0:T(8,128)S(1)}, f32[32,32]{1,0:T(8,128...) custom-call(f32[64,12,2,8,128]{4,3,2,1,0:T(8,128)} %bitcast.26, f32[64,12,2,8,128]{4,3,2,1,0:T(8,128)} %bitcast.27, ...), custom_call_target="tpu_custom_call" | custom-call | tf_op jit(solution)/shard_map/core/pallas_call | solution.py:404
  64.7 5.0 %finish.1 = (f32[32,12,2,8,128]{4,3,2,1,0:T(8,128)}, f32[32,12,2,8,128]{4,3,2,1,0:T(8,128)}, f32[32,12,2,8,128]{4,3,2,1,0:T(8,128)}, f32[32,12,2,8,128]{4,3,2,1,0:T(8,128)}, f32[32,32]{1,0:T(8,128)}) custom-call(f32[12,8,2,64,128]{4,3,2,1,0:T(8,128)S(1)} %get-tuple-element.16.new_ref, f32[12,8,2,64,128]{4,3,2,1,0:T(8,128)S(1)} %get-tuple-element.17.image_ref, ...), custom_call_target="tpu_custom_call" | custom-call | tf_op jit(solution)/shard_map/finish/pallas_call | solution.py:502
